TPU v7x, 128 devices: a whole 4x4x4 slice. The times are simulated.
128 devices in a mesh: gx: 8 (over z_lo, y), gy: 16 (over x, z_hi, core).
Axes of the slice: x: 4, y: 4, z: 4 (z_hi: 2, z_lo: 2; z = z_hi * 2 + z_lo), core: 2. Of those that a mesh axis runs over, the one named last changes fastest.
Arguments:
- initial_state: float32 [3, 256, 49152], P(None, 'gx', 'gy'), may hold values from -6 to 6
- beam_dir: float32 [3, 512], P(None, ('gx', 'gy')), may hold values from -4 to 4
- gate_obs: float32 [3, 128, 128, 32], P(None, ('gx', 'gy')), may hold values from -6 to 6
- slot_beam: int32 [128, 128, 32], P(('gx', 'gy')), may hold values from -1 to 3, as said below
- slot_cell: int32 [128, 128, 32], P(('gx', 'gy')), may hold values from 0 to 98303, as said below
Outputs:
- gradient: float32 [3, 256, 49152], P(None, 'gx', 'gy')
Inputs may be any that keep to these rules, and one draw needn't show every extreme that they name: `slot_beam`: each of an owner's 4 beams fills exactly 512 slots over all of that owner's lists. In every list the used slots come first. Each owner's list for one common tile is full, so that tile receives 32 used slots from every owner. `slot_cell`: A cell index within the tile, of 32 x 32 x 96 cells with the streamwise index slowest and the vertical fastest; empty slots also hold a valid index.
All inputs are finite; a program needn't handle non-finite values.
Results may differ from a plain program's by a relative error of at most 0.00015.
Values sent between devices are 32-bit elements; how exact they have to be, the bound alone decides.
A program may use at most 128 MiB of HBM per device.

v0:
```python
import jax
import jax.numpy as jnp
from jax import lax
from jax.experimental import pallas as pl
from jax.experimental.pallas import tpu as pltpu
from jax.sharding import PartitionSpec as P

NZ = 96
LANES = 128
GATES = 512
BEAMS = 4
STEPS = 3
TIME_STEP = 0.2
VISCOSITY = 0.5
HALF = 0.5 * TIME_STEP
CX = 32
CY = 32
TOP = 8
ROWS = CX + 2 * TOP
WIDE = CY + 2
COPIES = 2
MIB = 1024 * 1024
MESH = pl.DeviceIdType.MESH
VMEM = pl.BlockSpec(memory_space=pltpu.VMEM)
SMEM = pl.BlockSpec(memory_space=pltpu.SMEM)
INNER = (TOP + 8, TOP + 16)
OUTER = (TOP, TOP + 24)


def f32(*shape):
    return jax.ShapeDtypeStruct(shape, jnp.float32)


def sizes():
    return lax.axis_size("gx"), lax.axis_size("gy"), lax.axis_index("gx"), lax.axis_index("gy")


def shift_up(v):
    return pltpu.roll(v, LANES - 1, 1)


def shift_down(v):
    return pltpu.roll(v, 1, 1)


def levels():
    return lax.broadcasted_iota(jnp.int32, (8, LANES), 1) < NZ


def step_block(src, y, r):
    rows, fore, back = pl.ds(r, 8), pl.ds(r + 1, 8), pl.ds(r - 1, 8)
    centre = [src[c, y, rows, :] for c in range(3)]
    less = [1.0 - v for v in centre]
    more = [1.0 + v for v in centre]
    out = []
    for c in range(3):
        v = centre[c]
        total = src[c, y, fore, :] * less[0] + src[c, y, back, :] * more[0]
        total += src[c, y + 1, rows, :] * less[1] + src[c, y - 1, rows, :] * more[1]
        total += shift_up(v) * less[2] + shift_down(v) * more[2]
        out.append((1.0 - 6.0 * HALF) * v + HALF * total)
    return out


def pull_block(src, adj, y, r):
    rows, fore, back = pl.ds(r, 8), pl.ds(r + 1, 8), pl.ds(r - 1, 8)
    near = []
    for c in range(3):
        v = src[c, y, rows, :]
        near.append((src[c, y, fore, :], src[c, y, back, :], src[c, y + 1, rows, :], src[c, y - 1, rows, :],
                     shift_up(v), shift_down(v)))
    factors = [1.0 + near[0][0], 1.0 - near[0][1], 1.0 + near[1][2], 1.0 - near[1][3],
               1.0 + near[2][4], 1.0 - near[2][5]]
    a = [adj[c, y, rows, :] for c in range(3)]
    out = []
    for c in range(3):
        total = adj[c, y, fore, :] * factors[0] + adj[c, y, back, :] * factors[1]
        total += adj[c, y + 1, rows, :] * factors[2] + adj[c, y - 1, rows, :] * factors[3]
        total += shift_up(a[c]) * factors[4] + shift_down(a[c]) * factors[5]
        for k in range(3):
            total -= a[k] * (near[k][2 * c] - near[k][2 * c + 1])
        out.append((1.0 - 6.0 * HALF) * a[c] + HALF * total)
    return out


def pack_rims(field, sides):
    flat = field.reshape(3, WIDE * ROWS, LANES)
    for c in range(3):
        for y in range(0, CY, 8):
            at = pl.ds(y, 8)
            sides[0, c, at, :] = flat[c, pl.ds((y + 1) * ROWS + TOP, 8, stride=ROWS), :]
            sides[1, c, at, :] = flat[c, pl.ds((y + 1) * ROWS + TOP + CX - 1, 8, stride=ROWS), :]
            sides[2, c, at, :] = field[c, 1, pl.ds(TOP + y, 8), :]
            sides[3, c, at, :] = field[c, CY, pl.ds(TOP + y, 8), :]


def unpack_rims(field, sides, n_gx, n_gy, gx, gy):
    flat = field.reshape(3, WIDE * ROWS, LANES)
    inside = (gx < n_gx - 1, gx > 0, gy < n_gy - 1, gy > 0)
    for c in range(3):
        for y in range(0, CY, 8):
            v = [jnp.where(inside[s], sides[s, c, pl.ds(y, 8), :], 0.0) for s in range(4)]
            flat[c, pl.ds((y + 1) * ROWS + TOP + CX, 8, stride=ROWS), :] = v[0]
            flat[c, pl.ds((y + 1) * ROWS + TOP - 1, 8, stride=ROWS), :] = v[1]
            field[c, CY + 1, pl.ds(TOP + y, 8), :] = v[2]
            field[c, 0, pl.ds(TOP + y, 8), :] = v[3]


def send_rims(sides, inbox, send, recv, n_gx, n_gy, gx, gy):
    targets = (
        (lax.rem(gx + n_gx - 1, n_gx), gy), (lax.rem(gx + 1, n_gx), gy),
        (gx, lax.rem(gy + n_gy - 1, n_gy)), (gx, lax.rem(gy + 1, n_gy)),
    )
    copies = []
    for s, target in enumerate(targets):
        copy = pltpu.make_async_remote_copy(
            src_ref=sides.at[s], dst_ref=inbox.at[s], send_sem=send.at[s], recv_sem=recv.at[s],
            device_id=target, device_id_type=MESH,
        )
        copy.start()
        copies.append(copy)
    return copies


def over_tile(body, inner):
    if inner:
        def layer(y, carry):
            for r in INNER:
                body(y, r)
            return carry

        lax.fori_loop(2, CY, layer, 0)
        return

    def layer(y, carry):
        for r in OUTER:
            body(y, r)
        return carry

    lax.fori_loop(1, CY + 1, layer, 0)
    for y in (1, CY):
        for r in INNER:
            body(y, r)


def regroup(block, quantity):
    lane = lax.broadcasted_iota(jnp.int32, (32, LANES), 1)
    out = None
    for k in range(4):
        piece = block[32 * k : 32 * k + 32, :]
        turn = (32 * (k - quantity)) % LANES
        if turn:
            piece = pltpu.roll(piece, turn, 1)
        out = piece if out is None else jnp.where(lane >= 32 * k, piece, out)
    return out


def forward_kernel(
    state, cell, obs, beam, beam_dir,
    w0, w1, w2, tab_a, tab_b, packed, slots, seen_obs,
    got, msg, sides, inbox, send, recv, list_send, list_recv, own,
):
    n_gx, n_gy, gx, gy = sizes()
    count = n_gx * n_gy
    me = gx * n_gy + gy
    barrier = pltpu.get_barrier_semaphore()

    def device(i):
        peer = lax.rem(me + i, count)
        return peer, (peer // n_gy, lax.rem(peer, n_gy))

    def hail(i, carry):
        pl.semaphore_signal(barrier, inc=1, device_id=device(i)[1], device_id_type=MESH)
        return carry

    lax.fori_loop(1, count, hail, 0)
    kind = beam[...]
    heads = [cell[...].astype(jnp.float32), obs[0], obs[1], obs[2]]
    tails = [kind.astype(jnp.float32)]
    for c in range(3):
        weight = jnp.zeros(kind.shape, jnp.float32)
        for b in range(BEAMS):
            weight = jnp.where(kind == b, beam_dir[c, b], weight)
        tails.append(weight)
    msg[:, 0, :] = jnp.concatenate(heads, axis=0).T
    msg[:, 1, :] = jnp.concatenate(tails, axis=0).T

    lane = lax.broadcasted_iota(jnp.int32, (CX, LANES), 1)
    for c in range(3):
        for y in range(0, CY, 4):
            t = [state[c, :, pl.ds(y * NZ + LANES * i, LANES)] for i in range(3)]
            planes = [
                t[0],
                pltpu.roll(jnp.where(lane >= 96, t[0], t[1]), 32, 1),
                pltpu.roll(jnp.where(lane >= 64, t[1], t[2]), 64, 1),
                pltpu.roll(t[2], 96, 1),
            ]
            for i, v in enumerate(planes):
                w0[c, y + 1 + i, pl.ds(TOP, CX), :] = jnp.where(lane < NZ, v, 0.0)
    pack_rims(w0, sides.at[0])
    pl.semaphore_wait(barrier, count - 1)

    where = (n_gx, n_gy, gx, gy)
    copies = send_rims(sides.at[0], inbox.at[0], send.at[0], recv.at[0], *where)

    def post(i, carry):
        peer, target = device(i)
        pltpu.make_async_remote_copy(
            src_ref=msg.at[peer], dst_ref=got.at[me], send_sem=list_send, recv_sem=list_recv,
            device_id=target, device_id_type=MESH,
        ).start()
        return carry

    lax.fori_loop(1, count, post, 0)
    mine = pltpu.make_async_copy(msg.at[me], got.at[me], own)
    mine.start()

    keep = levels()

    def advance(src, dst):
        def body(y, r):
            for c, v in enumerate(step_block(src, y, r)):
                dst[c, y, pl.ds(r, 8), :] = jnp.where(keep, v, 0.0)
        return body

    def tables(y, r):
        at = ((y - 1) * CX + (r - TOP)) * 8
        for c, v in enumerate(step_block(w2, y, r)):
            tab_a[pl.ds(at + c, 8, stride=8), :] = v
            tab_a[pl.ds(at + 3 + c, 8, stride=8), :] = w2[c, y, pl.ds(r, 8), :]
            tab_b[pl.ds(at + c, 8, stride=8), :] = w1[c, y, pl.ds(r, 8), :]

    for n, (src, body) in enumerate(((w0, advance(w0, w1)), (w1, advance(w1, w2)), (w2, tables))):
        if n:
            pack_rims(src, sides.at[n])
            copies = send_rims(sides.at[n], inbox.at[n], send.at[n], recv.at[n], *where)
        over_tile(body, True)
        for copy in copies:
            copy.wait()
        unpack_rims(src, inbox.at[n], *where)
        over_tile(body, False)

    mine.wait()
    rest = pl.ds(0, count - 1)
    pltpu.make_async_remote_copy(
        src_ref=msg.at[rest], dst_ref=got.at[rest], send_sem=list_send, recv_sem=list_recv,
        device_id=device(1)[1], device_id_type=MESH,
    ).wait()
    g0, g1 = got[:, 0, :], got[:, 1, :]
    where_to = regroup(g0, 0).astype(jnp.int32)
    x = ((where_to >> 10) * 171) >> 9
    rem = where_to - x * (CY * NZ)
    y = ((rem >> 5) * 171) >> 9
    z = rem - y * NZ
    lane = lax.broadcasted_iota(jnp.int32, (32, LANES), 1)
    packed[...] = (y * CX + x) * LANES + ((lane - z) & (LANES - 1))
    for j in range(4):
        slots[j] = regroup(g1, j)
    for n in range(STEPS):
        seen_obs[n] = regroup(g0, 1 + n)


def forward(state, cell, obs, beam, beam_dir):
    count = cell.shape[1]
    wide, table = f32(3, WIDE, ROWS, LANES), f32(CX * CY * 8, LANES)
    rim = pltpu.VMEM((STEPS, 4, 3, 32, LANES), jnp.float32)
    return pl.pallas_call(
        forward_kernel,
        out_shape=[wide, wide, wide, table, table, jax.ShapeDtypeStruct((32, LANES), jnp.int32), f32(4, 32, LANES), f32(STEPS, 32, LANES)],
        in_specs=[VMEM] * 4 + [SMEM],
        out_specs=[VMEM] * 8,
        scratch_shapes=[
            pltpu.VMEM((count, 2, LANES), jnp.float32), pltpu.VMEM((count, 2, LANES), jnp.float32), rim, rim,
            pltpu.SemaphoreType.DMA((STEPS, 4)), pltpu.SemaphoreType.DMA((STEPS, 4)),
            pltpu.SemaphoreType.DMA, pltpu.SemaphoreType.DMA, pltpu.SemaphoreType.DMA,
        ],
        compiler_params=pltpu.CompilerParams(collective_id=0, has_side_effects=True, vmem_limit_bytes=24 * MIB),
        name="forward",
    )(state, cell, obs, beam, beam_dir)


def same_list():
    a = lax.broadcasted_iota(jnp.int32, (LANES, LANES), 0) >> 5
    b = lax.broadcasted_iota(jnp.int32, (LANES, LANES), 1) >> 5
    return (a == b).astype(jnp.float32)


def diagonal():
    g = lax.broadcasted_iota(jnp.int32, (32, LANES), 0)
    lane = lax.broadcasted_iota(jnp.int32, (32, LANES), 1)
    return (lane & 31) == g


def list_sums(values):
    return jnp.dot(
        jnp.concatenate(values, axis=0), same_list(), precision=lax.Precision.HIGHEST,
        preferred_element_type=jnp.float32,
    )


def gather_kernel(
    index, tab_a, tab_b, slots, seen_obs,
    resid, part,
    acc_a, acc_b,
):
    part[...] = jnp.zeros_like(part)

    lane8 = lax.broadcasted_iota(jnp.int32, (8, LANES), 1)

    def pick(g, carry):
        a = jnp.zeros((8, LANES), jnp.float32)
        b = jnp.zeros((8, LANES), jnp.float32)
        for j in range(LANES):
            code = index[g, j]
            at = pl.multiple_of((code >> 7) * 8, 8)
            turn = code & (LANES - 1)
            here = lane8 == j
            a = jnp.where(here, pltpu.roll(tab_a[pl.ds(at, 8), :], turn, 1), a)
            b = jnp.where(here, pltpu.roll(tab_b[pl.ds(at, 8), :], turn, 1), b)
        at = pl.multiple_of(g * 8, 8)
        acc_a[pl.ds(at, 8), :] = a
        acc_b[pl.ds(at, 8), :] = b
        return carry

    lax.fori_loop(0, 32, pick, 0)

    diag = diagonal()
    beam = slots[0]
    values = []
    for n in range(STEPS):
        ref, base = ((acc_b, 0), (acc_a, 3), (acc_a, 0))[n]
        seen = sum(slots[1 + c] * ref[pl.ds(base + c, 32, stride=8), :] for c in range(3))
        r = seen - seen_obs[n]
        resid[n] = r
        for b in range(BEAMS):
            values.append(jnp.where(beam == float(b), r, 0.0))
    sums = list_sums(values)
    for i in range(STEPS * BEAMS):
        block = jnp.where(diag, sums[32 * i : 32 * i + 32, :], 0.0)
        part[pl.ds(i, 1), :] = jnp.sum(block, axis=0, keepdims=True)

def gather(index, tab_a, tab_b, slots, seen_obs):
    rows = pltpu.VMEM((256, LANES), jnp.float32)
    return pl.pallas_call(
        gather_kernel,
        out_shape=[f32(STEPS, 32, LANES), f32(16, LANES)],
        in_specs=[SMEM] + [VMEM] * 4,
        out_specs=[VMEM] * 2,
        scratch_shapes=[rows, rows],
        compiler_params=pltpu.CompilerParams(vmem_limit_bytes=16 * MIB),
        name="gather",
    )(index, tab_a, tab_b, slots, seen_obs)


def misfit_kernel(
    part, resid, slots, vals_a, vals_b, half, inbox_a, inbox_b, send_a, recv_a, send_b, recv_b
):
    gx, gy = lax.axis_index("gx"), lax.axis_index("gy")
    q = (gx // 4) * 4 + lax.rem(gy, 4)
    p = lax.rem(gx, 4) * 4 + gy // 4

    def near(d):
        to = lax.rem(q + d, 8)
        return ((to // 4) * 4 + lax.rem(gx, 4), (gy // 4) * 4 + lax.rem(to, 4))

    def far(d):
        to = lax.rem(p + d, 16)
        return ((gx // 4) * 4 + to // 4, lax.rem(to, 4) * 4 + lax.rem(gy, 4))

    barrier = pltpu.get_barrier_semaphore()
    for d in range(1, 8):
        pl.semaphore_signal(barrier, inc=1, device_id=near(d), device_id_type=MESH)
    for d in range(1, 16):
        pl.semaphore_signal(barrier, inc=1, device_id=far(d), device_id_type=MESH)

    vals_a[...] = jnp.zeros_like(vals_a)
    vals_b[...] = jnp.zeros_like(vals_b)
    diag = diagonal()
    beam = slots[0]
    pl.semaphore_wait(barrier, 22)

    def spread(src, inbox, send, recv, where_to, peers):
        copies = []
        for d in range(1, peers):
            copy = pltpu.make_async_remote_copy(
                src_ref=src, dst_ref=inbox.at[d - 1], send_sem=send.at[d - 1], recv_sem=recv.at[d - 1],
                device_id=where_to(d), device_id_type=MESH,
            )
            copy.start()
            copies.append(copy)
        for copy in copies:
            copy.wait()

    spread(part, inbox_a, send_a, recv_a, near, 8)
    acc = part[...]
    for d in range(7):
        acc = acc + inbox_a[d]
    half[...] = acc
    spread(half, inbox_b, send_b, recv_b, far, 16)
    for d in range(15):
        acc = acc + inbox_b[d]

    total = acc * (1.0 / GATES)
    means = list_sums([jnp.where(diag, total[i : i + 1, :], 0.0) for i in range(STEPS * BEAMS)])
    for n in range(STEPS):
        at = 32 * BEAMS * n
        mean = jnp.zeros((32, LANES), jnp.float32)
        for b in range(BEAMS):
            mean = jnp.where(beam == float(b), means[at + 32 * b : at + 32 * b + 32, :], mean)
        misfit = jnp.where(beam >= 0.0, resid[n] - mean, 0.0)
        ref, base = ((vals_b, 0), (vals_a, 3), (vals_a, 0))[n]
        for c in range(3):
            ref[pl.ds(base + c, 32, stride=8), :] = slots[1 + c] * misfit


def misfits(part, resid, slots):
    return pl.pallas_call(
        misfit_kernel,
        out_shape=[f32(256, LANES), f32(256, LANES)],
        in_specs=[VMEM] * 3,
        out_specs=[VMEM] * 2,
        scratch_shapes=[
            pltpu.VMEM((16, LANES), jnp.float32),
            pltpu.VMEM((7, 16, LANES), jnp.float32), pltpu.VMEM((15, 16, LANES), jnp.float32),
            pltpu.SemaphoreType.DMA((7,)), pltpu.SemaphoreType.DMA((7,)),
            pltpu.SemaphoreType.DMA((15,)), pltpu.SemaphoreType.DMA((15,)),
        ],
        compiler_params=pltpu.CompilerParams(collective_id=1, has_side_effects=True, vmem_limit_bytes=16 * MIB),
        name="misfits",
    )(part, resid, slots)


def scatter_kernel(index, vals_a, vals_b, f3, f2, f1, *sums):
    blank = jnp.zeros((64, LANES), jnp.float32)

    def clear(i, carry):
        for ref in sums:
            ref[pl.ds(pl.multiple_of(i * 64, 64), 64), :] = blank
        return carry

    lax.fori_loop(0, CX * CY * 8 // 64, clear, 0)
    lane8 = lax.broadcasted_iota(jnp.int32, (8, LANES), 1)
    sum_a, sum_b = sums[:COPIES], sums[COPIES:]

    def place(g, carry):
        at = pl.multiple_of(g * 8, 8)
        va = vals_a[pl.ds(at, 8), :]
        vb = vals_b[pl.ds(at, 8), :]
        for j in range(LANES):
            code = index[g, j]
            to = pl.ds(pl.multiple_of((code >> 7) * 8, 8), 8)
            turn = (0 - code) & (LANES - 1)
            here = lane8 == ((j - code) & (LANES - 1))
            a, b = sum_a[j % COPIES], sum_b[j % COPIES]
            a[to, :] = a[to, :] + jnp.where(here, pltpu.roll(va, turn, 1), 0.0)
            b[to, :] = b[to, :] + jnp.where(here, pltpu.roll(vb, turn, 1), 0.0)
        return carry

    lax.fori_loop(0, 32, place, 0)

    def unpack(y, carry):
        for r in range(0, CX, 8):
            for out, refs, base in ((f3, sum_a, 0), (f2, sum_a, 3), (f1, sum_b, 0)):
                for c in range(3):
                    at = pl.ds((y * CX + r) * 8 + base + c, 8, stride=8)
                    out[c, y, pl.ds(r, 8), :] = sum(ref[at, :] for ref in refs)
        return carry

    lax.fori_loop(0, CY, unpack, 0)


def scatter(index, vals_a, vals_b):
    table = pltpu.VMEM((CX * CY * 8, LANES), jnp.float32)
    field = f32(3, CY, CX, LANES)
    return pl.pallas_call(
        scatter_kernel,
        out_shape=[field, field, field],
        in_specs=[SMEM, VMEM, VMEM],
        out_specs=[VMEM] * 3,
        scratch_shapes=[table] * (2 * COPIES),
        compiler_params=pltpu.CompilerParams(vmem_limit_bytes=32 * MIB),
        name="scatter",
    )(index, vals_a, vals_b)


def adjoint_kernel(w0, w1, w2, f3, f2, f1, out, a3, a2, a1, sides, inbox, send, recv):
    n_gx, n_gy, gx, gy = sizes()
    where = (n_gx, n_gy, gx, gy)
    barrier = pltpu.get_barrier_semaphore()
    for target in (
        (lax.rem(gx + n_gx - 1, n_gx), gy), (lax.rem(gx + 1, n_gx), gy),
        (gx, lax.rem(gy + n_gy - 1, n_gy)), (gx, lax.rem(gy + 1, n_gy)),
    ):
        pl.semaphore_signal(barrier, inc=1, device_id=target, device_id_type=MESH)

    def fill(y, carry):
        for c in range(3):
            a3[c, y + 1, pl.ds(TOP, CX), :] = f3[c, y]
        return carry

    lax.fori_loop(0, CY, fill, 0)
    keep = levels()

    def pull(src, adj, dst, force):
        def body(y, r):
            for c, v in enumerate(pull_block(src, adj, y, r)):
                v = jnp.where(keep, v, 0.0)
                if force is not None:
                    v = v + force[c, y - 1, pl.ds(r - TOP, 8), :]
                dst[c, y, pl.ds(r, 8), :] = v
        return body

    for n, (src, adj, dst, force) in enumerate(((w2, a3, a2, f2), (w1, a2, a1, f1), (w0, a1, a3, None))):
        body = pull(src, adj, dst, force)
        pack_rims(adj, sides.at[n])
        if n == 0:
            pl.semaphore_wait(barrier, 4)
        copies = send_rims(sides.at[n], inbox.at[n], send.at[n], recv.at[n], *where)
        over_tile(body, True)
        for copy in copies:
            copy.wait()
        unpack_rims(adj, inbox.at[n], *where)
        over_tile(body, False)

    lane = lax.broadcasted_iota(jnp.int32, (CX, LANES), 1)
    for c in range(3):
        for y in range(0, CY, 4):
            v = [a3[c, y + 1 + i, pl.ds(TOP, CX), :] for i in range(4)]
            v = [v[0], pltpu.roll(v[1], 96, 1), pltpu.roll(v[2], 64, 1), pltpu.roll(v[3], 32, 1)]
            t = [
                jnp.where(lane < 96, v[0], v[1]),
                jnp.where(lane < 64, v[1], v[2]),
                jnp.where(lane < 32, v[2], v[3]),
            ]
            for i in range(3):
                out[c, :, pl.ds(y * NZ + LANES * i, LANES)] = t[i]


def adjoint(wides, fields):
    wide = pltpu.VMEM((3, WIDE, ROWS, LANES), jnp.float32)
    rim = pltpu.VMEM((STEPS, 4, 3, 32, LANES), jnp.float32)
    return pl.pallas_call(
        adjoint_kernel,
        out_shape=f32(3, CX, CY * NZ),
        in_specs=[VMEM] * 6,
        out_specs=VMEM,
        scratch_shapes=[wide] * 3 + [
            rim, rim, pltpu.SemaphoreType.DMA((STEPS, 4)), pltpu.SemaphoreType.DMA((STEPS, 4)),
        ],
        compiler_params=pltpu.CompilerParams(collective_id=2, has_side_effects=True, vmem_limit_bytes=24 * MIB),
        name="adjoint",
    )(*wides, *fields)


def local(initial_state, beam_dir, gate_obs, slot_beam, slot_cell):
    w0, w1, w2, tab_a, tab_b, index, slots, seen_obs = forward(
        initial_state, slot_cell[0].T, jnp.transpose(gate_obs[:, 0], (0, 2, 1)), slot_beam[0].T, beam_dir
    )
    resid, part = gather(index, tab_a, tab_b, slots, seen_obs)
    vals_a, vals_b = misfits(part, resid, slots)
    fields = scatter(index, vals_a, vals_b)
    return adjoint((w0, w1, w2), fields)


def solution(mesh):
    in_specs = (
        P(None, "gx", "gy"),
        P(None, ("gx", "gy")),
        P(None, ("gx", "gy"), None, None),
        P(("gx", "gy"), None, None),
        P(("gx", "gy"), None, None),
    )
    out_specs = P(None, "gx", "gy")
    return jax.shard_map(local, mesh=mesh, in_specs=in_specs, out_specs=out_specs, check_vma=False)
```

profile of v0, /device:TPU:0, one launch (start us, length us, event | category | flops | bytes accessed | tf_op | source)
XLA Modules:
  0.0 110.3 jit_solution(15953714321687129227)
XLA Ops:
  0.0 0.0 copy-start
  0.0 1.3 %copy-done = f32[3,32,3072]{2,1,0:T(8,128)S(1)} copy-done((f32[3,32,3072]{2,1,0:T(8,128)S(1)}, f32[3,32,3072]{2,1,0:T(8,128)}, u32[]{:S(2)}) %copy-start) | copy-done | bytes 1179672
  1.3 0.0 copy-start.1
  1.3 0.8 copy-done.1
  2.1 0.0 copy-start.2
  2.1 0.7 copy-done.2
  2.8 0.0 copy-start.3
  2.8 0.7 copy-done.3
  3.5 0.0 copy-start.4
  3.5 0.7 copy-done.4
  4.2 34.9 %forward.1 = (f32[3,34,48,128]{3,2,1,0:T(8,128)S(1)}, f32[3,34,48,128]{3,2,1,0:T(8,128)S(1)}, f32[3,34,48,128]{3,2,1,0:T(8,128)S(1)}, f32[8192,128]{1,0:T(8,128)...) custom-call(f32[3,32,3072]{2,1,0:T(8,128)S(1)} %copy-done, ...), custom_call_target="tpu_custom_call" | custom-call | tf_op jit(solution)/shard_map/forward/pallas_call | solution.py:267
  39.1 12.1 %gather.1 = (f32[3,32,128]{2,1,0:T(8,128)S(1)}, f32[16,128]{1,0:T(8,128)S(1)}) custom-call(s32[32,128]{1,0:T(8,128)S(1)} %get-tuple-element.23.index, f32[8192,128]{1,0:T(8,128)S(1)} %get-tuple-element.24.tab_a, f32[8192,128]{1,0:T(8,128)S(1)} %get-tuple-element.25.tab_b, f32[4,32,128]{2,1,0:T(8,128)S(1)} %get-tuple-element.26.slots, ...), custom_call_target="tpu_custom_call" | custom-call | tf_op jit(solution)/shard_map/gather/pallas_call | solution.py:344
  51.2 13.0 %misfits.1 = (f32[256,128]{1,0:T(8,128)S(1)}, f32[256,128]{1,0:T(8,128)S(1)}) custom-call(f32[16,128]{1,0:T(8,128)S(1)} %get-tuple-element.28.part, f32[3,32,128]{2,1,0:T(8,128)S(1)} %get-tuple-element.29.resid, f32[4,32,128]{2,1,0:T(8,128)S(1)} %get-tuple-element.26.slots), custom_call_target="tpu_custom_call" | custom-call | tf_op jit(solution)/shard_map/misfits/pallas_call | solution.py:417
  64.2 17.5 %scatter.1 = (f32[3,32,32,128]{3,2,1,0:T(8,128)S(1)}, f32[3,32,32,128]{3,2,1,0:T(8,128)S(1)}, f32[3,32,32,128]{3,2,1,0:T(8,128)S(1)}) custom-call(s32[32,128]{1,0:T(8,128)S(1)} %get-tuple-element.23.index, f32[256,128]{1,0:T(8,128)S(1)} %get-tuple-element.30.vals_a, f32[256,128]{1,0:T(8,128)S(1)} %get-tuple-element.31.vals_b), custom_call_target="tpu_custom_call" | custom-call | tf_op jit(solution)/shard_map/scatter/pallas_call | solution.py:475
  81.7 27.6 %adjoint.1 = f32[3,32,3072]{2,1,0:T(8,128)S(1)} custom-call(f32[3,34,48,128]{3,2,1,0:T(8,128)S(1)} %get-tuple-element.20.w0, f32[3,34,48,128]{3,2,1,0:T(8,128)S(1)} %get-tuple-element.21.w1, f32[3,34,48,128]{3,2,1,0:T(8,128)S(1)} %get-tuple-element.22.w2, f32[3,32,32,128]{3,2,1,0:T(8,128)S(1)} %get-tuple-element.32.f3, ...), custom_call_target="tpu_custom_call" | custom-call | tf_op jit(solution)/shard_map/adjoint/pallas_call | solution.py:542
  109.3 1.0 copy.7
Async XLA Ops:
  0.0 1.3 %copy-start = (f32[3,32,3072]{2,1,0:T(8,128)S(1)}, f32[3,32,3072]{2,1,0:T(8,128)}, u32[]{:S(2)}) copy-start(f32[3,32,3072]{2,1,0:T(8,128)} %state.1) | copy-start | bytes 3538948
  1.3 0.8 copy-start.1
  2.1 0.7 copy-start.2
  2.8 0.7 copy-start.3
  3.5 0.7 copy-start.4
where the time goes:
time: 111 us; the launch traced here: 110 us
  Pallas kernels  105 us (95%)
  local copies, waits for them, and re-layouts  5.2 us (5%)
    pallas_call x1, Pallas kernels, forward(): pl.pallas_call(forward_kernel, out_shape=[wide, wide, wide, table, table,...  34.9 us
    pallas_call x1, Pallas kernels, adjoint(): pl.pallas_call(adjoint_kernel, out_shape=f32(3, CX, CY * NZ), in_specs=[V...  27.6 us
    pallas_call x1, Pallas kernels, scatter(): pl.pallas_call(scatter_kernel, out_shape=[field, field, field], in_specs=...  17.5 us
    pallas_call x1, Pallas kernels, misfits(): pl.pallas_call(misfit_kernel, out_shape=[f32(256, LANES), f32(256, LANES)...  13 us
    pallas_call x1, Pallas kernels, gather(): pl.pallas_call(gather_kernel, out_shape=[f32(STEPS, 32, LANES), f32(16, L...  12.1 us
    unnamed x11, local copies, waits for them, and re-layouts  5.2 us

commit v1 on v0

--- a/solution.py
+++ b/solution.py
@@ -19,12 +19,12 @@
 ROWS = CX + 2 * TOP
 WIDE = CY + 2
 COPIES = 2
+TILE = 16
+UNROLL = 4
 MIB = 1024 * 1024
 MESH = pl.DeviceIdType.MESH
 VMEM = pl.BlockSpec(memory_space=pltpu.VMEM)
 SMEM = pl.BlockSpec(memory_space=pltpu.SMEM)
-INNER = (TOP + 8, TOP + 16)
-OUTER = (TOP, TOP + 24)
 
 
 def f32(*shape):
@@ -83,29 +83,6 @@
     return out
 
 
-def pack_rims(field, sides):
-    flat = field.reshape(3, WIDE * ROWS, LANES)
-    for c in range(3):
-        for y in range(0, CY, 8):
-            at = pl.ds(y, 8)
-            sides[0, c, at, :] = flat[c, pl.ds((y + 1) * ROWS + TOP, 8, stride=ROWS), :]
-            sides[1, c, at, :] = flat[c, pl.ds((y + 1) * ROWS + TOP + CX - 1, 8, stride=ROWS), :]
-            sides[2, c, at, :] = field[c, 1, pl.ds(TOP + y, 8), :]
-            sides[3, c, at, :] = field[c, CY, pl.ds(TOP + y, 8), :]
-
-
-def unpack_rims(field, sides, n_gx, n_gy, gx, gy):
-    flat = field.reshape(3, WIDE * ROWS, LANES)
-    inside = (gx < n_gx - 1, gx > 0, gy < n_gy - 1, gy > 0)
-    for c in range(3):
-        for y in range(0, CY, 8):
-            v = [jnp.where(inside[s], sides[s, c, pl.ds(y, 8), :], 0.0) for s in range(4)]
-            flat[c, pl.ds((y + 1) * ROWS + TOP + CX, 8, stride=ROWS), :] = v[0]
-            flat[c, pl.ds((y + 1) * ROWS + TOP - 1, 8, stride=ROWS), :] = v[1]
-            field[c, CY + 1, pl.ds(TOP + y, 8), :] = v[2]
-            field[c, 0, pl.ds(TOP + y, 8), :] = v[3]
-
-
 def send_rims(sides, inbox, send, recv, n_gx, n_gy, gx, gy):
     targets = (
         (lax.rem(gx + n_gx - 1, n_gx), gy), (lax.rem(gx + 1, n_gx), gy),
@@ -122,25 +99,53 @@
     return copies
 
 
-def over_tile(body, inner):
-    if inner:
-        def layer(y, carry):
-            for r in INNER:
-                body(y, r)
-            return carry
-
-        lax.fori_loop(2, CY, layer, 0)
-        return
-
+def over_tile(body):
     def layer(y, carry):
-        for r in OUTER:
+        for r in range(TOP, TOP + CX, 8):
             body(y, r)
         return carry
 
+    lax.fori_loop(1, CY + 1, layer, 0, unroll=UNROLL)
+
+
+def clear_rims(fields):
+    blank = jnp.zeros((8, LANES), jnp.float32)
+
+    def layer(y, carry):
+        for field in fields:
+            for c in range(3):
+                field[c, y, pl.ds(0, 8), :] = blank
+                field[c, y, pl.ds(TOP + CX, 8), :] = blank
+        return carry
+
     lax.fori_loop(1, CY + 1, layer, 0)
-    for y in (1, CY):
-        for r in INNER:
-            body(y, r)
+    for field in fields:
+        for c in range(3):
+            for y in (0, CY + 1):
+                for r in range(TOP, TOP + CX, 8):
+                    field[c, y, pl.ds(r, 8), :] = blank
+
+
+def layer_at(field, side, depth, c, y):
+    if side < 2:
+        row = TOP - depth if side == 0 else TOP + CX - 1 + depth
+        return field.reshape(3, WIDE * ROWS, LANES), (c, pl.ds((y + 1) * ROWS + row, 8, stride=ROWS), slice(None))
+    return field, (c, 1 - depth if side == 2 else CY + depth, pl.ds(TOP + y, 8), slice(None))
+
+
+OPPOSITE = (1, 0, 3, 2)
+
+
+def inside_grid(n_gx, n_gy, gx, gy):
+    return (gx > 0, gx < n_gx - 1, gy > 0, gy < n_gy - 1)
+
+
+def pack_rims(field, sides):
+    for s in range(4):
+        for c in range(3):
+            for y in range(0, CY, 8):
+                ref, at = layer_at(field, s, 0, c, y)
+                sides[s, c, pl.ds(y, 8), :] = ref[at]
 
 
 def regroup(block, quantity):
@@ -157,7 +162,7 @@
 
 def forward_kernel(
     state, cell, obs, beam, beam_dir,
-    w0, w1, w2, tab_a, tab_b, packed, slots, seen_obs,
+    w0, w1, w2, table, take, give, slots, seen_obs,
     got, msg, sides, inbox, send, recv, list_send, list_recv, own,
 ):
     n_gx, n_gy, gx, gy = sizes()
@@ -198,6 +203,7 @@
             for i, v in enumerate(planes):
                 w0[c, y + 1 + i, pl.ds(TOP, CX), :] = jnp.where(lane < NZ, v, 0.0)
     pack_rims(w0, sides.at[0])
+    clear_rims((w0, w1, w2))
     pl.semaphore_wait(barrier, count - 1)
 
     where = (n_gx, n_gy, gx, gy)
@@ -223,22 +229,45 @@
                 dst[c, y, pl.ds(r, 8), :] = jnp.where(keep, v, 0.0)
         return body
 
+    cells = table.reshape(CX * CY * TILE, LANES)
+
     def tables(y, r):
-        at = ((y - 1) * CX + (r - TOP)) * 8
+        at = ((y - 1) * CX + (r - TOP)) * TILE
         for c, v in enumerate(step_block(w2, y, r)):
-            tab_a[pl.ds(at + c, 8, stride=8), :] = v
-            tab_a[pl.ds(at + 3 + c, 8, stride=8), :] = w2[c, y, pl.ds(r, 8), :]
-            tab_b[pl.ds(at + c, 8, stride=8), :] = w1[c, y, pl.ds(r, 8), :]
-
-    for n, (src, body) in enumerate(((w0, advance(w0, w1)), (w1, advance(w1, w2)), (w2, tables))):
+            cells[pl.ds(at + c, 8, stride=TILE), :] = v
+            cells[pl.ds(at + 3 + c, 8, stride=TILE), :] = w2[c, y, pl.ds(r, 8), :]
+            cells[pl.ds(at + 8 + c, 8, stride=TILE), :] = w1[c, y, pl.ds(r, 8), :]
+
+    def target(dst, s, c, y):
+        if dst is not None:
+            return layer_at(dst, s, 0, c, y)
+        if s < 2:
+            return cells, (pl.ds((y * CX + (CX - 1) * s) * TILE + c, 8, stride=CX * TILE), slice(None))
+        return cells, (pl.ds(((CY - 1) * (s - 2) * CX + y) * TILE + c, 8, stride=TILE), slice(None))
+
+    inside = inside_grid(*where)
+
+    def meet_rims(src, dst, n):
+        for s in range(4):
+            for y in range(0, CY, 8):
+                rows = pl.ds(y, 8)
+                speed = sides[n, s, s // 2, rows, :]
+                factor = HALF * (1.0 - speed) if s % 2 else HALF * (1.0 + speed)
+                for c in range(3):
+                    v = jnp.where(inside[s], inbox[n, OPPOSITE[s], c, rows, :], 0.0)
+                    ref, at = layer_at(src, s, 1, c, y)
+                    ref[at] = v
+                    ref, at = target(dst, s, c, y)
+                    ref[at] = ref[at] + factor * v
+
+    for n, (src, dst, body) in enumerate(((w0, w1, advance(w0, w1)), (w1, w2, advance(w1, w2)), (w2, None, tables))):
         if n:
             pack_rims(src, sides.at[n])
             copies = send_rims(sides.at[n], inbox.at[n], send.at[n], recv.at[n], *where)
-        over_tile(body, True)
+        over_tile(body)
         for copy in copies:
             copy.wait()
-        unpack_rims(src, inbox.at[n], *where)
-        over_tile(body, False)
+        meet_rims(src, dst, n)
 
     mine.wait()
     rest = pl.ds(0, count - 1)
@@ -253,7 +282,9 @@
     y = ((rem >> 5) * 171) >> 9
     z = rem - y * NZ
     lane = lax.broadcasted_iota(jnp.int32, (32, LANES), 1)
-    packed[...] = (y * CX + x) * LANES + ((lane - z) & (LANES - 1))
+    at = (y * CX + x) * (TILE * LANES)
+    take[...] = at + ((lane - z) & (LANES - 1))
+    give[...] = at + ((z - lane) & (LANES - 1))
     for j in range(4):
         slots[j] = regroup(g1, j)
     for n in range(STEPS):
@@ -262,11 +293,12 @@
 
 def forward(state, cell, obs, beam, beam_dir):
     count = cell.shape[1]
-    wide, table = f32(3, WIDE, ROWS, LANES), f32(CX * CY * 8, LANES)
+    wide, table = f32(3, WIDE, ROWS, LANES), f32(CX * CY, TILE, LANES)
+    codes = jax.ShapeDtypeStruct((32, LANES), jnp.int32)
     rim = pltpu.VMEM((STEPS, 4, 3, 32, LANES), jnp.float32)
     return pl.pallas_call(
         forward_kernel,
-        out_shape=[wide, wide, wide, table, table, jax.ShapeDtypeStruct((32, LANES), jnp.int32), f32(4, 32, LANES), f32(STEPS, 32, LANES)],
+        out_shape=[wide, wide, wide, table, codes, codes, f32(4, 32, LANES), f32(STEPS, 32, LANES)],
         in_specs=[VMEM] * 4 + [SMEM],
         out_specs=[VMEM] * 8,
         scratch_shapes=[
@@ -299,10 +331,30 @@
 
 
 def gather_kernel(
-    index, tab_a, tab_b, slots, seen_obs,
-    resid, part,
-    acc_a, acc_b,
+    take, table, slots, seen_obs,
+    vals_a, vals_b,
+    acc_a, acc_b, resid, part, half, inbox_a, inbox_b, send_a, recv_a, send_b, recv_b,
 ):
+    gx, gy = lax.axis_index("gx"), lax.axis_index("gy")
+    q = (gx // 4) * 4 + lax.rem(gy, 4)
+    p = lax.rem(gx, 4) * 4 + gy // 4
+
+    def near(d):
+        to = lax.rem(q + d, 8)
+        return ((to // 4) * 4 + lax.rem(gx, 4), (gy // 4) * 4 + lax.rem(to, 4))
+
+    def far(d):
+        to = lax.rem(p + d, 16)
+        return ((gx // 4) * 4 + to // 4, lax.rem(to, 4) * 4 + lax.rem(gy, 4))
+
+    barrier = pltpu.get_barrier_semaphore()
+    for d in range(1, 8):
+        pl.semaphore_signal(barrier, inc=1, device_id=near(d), device_id_type=MESH)
+    for d in range(1, 16):
+        pl.semaphore_signal(barrier, inc=1, device_id=far(d), device_id_type=MESH)
+
+    vals_a[...] = jnp.zeros_like(vals_a)
+    vals_b[...] = jnp.zeros_like(vals_b)
     part[...] = jnp.zeros_like(part)
 
     lane8 = lax.broadcasted_iota(jnp.int32, (8, LANES), 1)
@@ -311,12 +363,11 @@
         a = jnp.zeros((8, LANES), jnp.float32)
         b = jnp.zeros((8, LANES), jnp.float32)
         for j in range(LANES):
-            code = index[g, j]
-            at = pl.multiple_of((code >> 7) * 8, 8)
-            turn = code & (LANES - 1)
+            code = take[g, j]
+            tile = pltpu.roll(table[code >> 11], code & (LANES - 1), 1)
             here = lane8 == j
-            a = jnp.where(here, pltpu.roll(tab_a[pl.ds(at, 8), :], turn, 1), a)
-            b = jnp.where(here, pltpu.roll(tab_b[pl.ds(at, 8), :], turn, 1), b)
+            a = jnp.where(here, tile[:8], a)
+            b = jnp.where(here, tile[8:], b)
         at = pl.multiple_of(g * 8, 8)
         acc_a[pl.ds(at, 8), :] = a
         acc_b[pl.ds(at, 8), :] = b
@@ -338,45 +389,6 @@
     for i in range(STEPS * BEAMS):
         block = jnp.where(diag, sums[32 * i : 32 * i + 32, :], 0.0)
         part[pl.ds(i, 1), :] = jnp.sum(block, axis=0, keepdims=True)
-
-def gather(index, tab_a, tab_b, slots, seen_obs):
-    rows = pltpu.VMEM((256, LANES), jnp.float32)
-    return pl.pallas_call(
-        gather_kernel,
-        out_shape=[f32(STEPS, 32, LANES), f32(16, LANES)],
-        in_specs=[SMEM] + [VMEM] * 4,
-        out_specs=[VMEM] * 2,
-        scratch_shapes=[rows, rows],
-        compiler_params=pltpu.CompilerParams(vmem_limit_bytes=16 * MIB),
-        name="gather",
-    )(index, tab_a, tab_b, slots, seen_obs)
-
-
-def misfit_kernel(
-    part, resid, slots, vals_a, vals_b, half, inbox_a, inbox_b, send_a, recv_a, send_b, recv_b
-):
-    gx, gy = lax.axis_index("gx"), lax.axis_index("gy")
-    q = (gx // 4) * 4 + lax.rem(gy, 4)
-    p = lax.rem(gx, 4) * 4 + gy // 4
-
-    def near(d):
-        to = lax.rem(q + d, 8)
-        return ((to // 4) * 4 + lax.rem(gx, 4), (gy // 4) * 4 + lax.rem(to, 4))
-
-    def far(d):
-        to = lax.rem(p + d, 16)
-        return ((gx // 4) * 4 + to // 4, lax.rem(to, 4) * 4 + lax.rem(gy, 4))
-
-    barrier = pltpu.get_barrier_semaphore()
-    for d in range(1, 8):
-        pl.semaphore_signal(barrier, inc=1, device_id=near(d), device_id_type=MESH)
-    for d in range(1, 16):
-        pl.semaphore_signal(barrier, inc=1, device_id=far(d), device_id_type=MESH)
-
-    vals_a[...] = jnp.zeros_like(vals_a)
-    vals_b[...] = jnp.zeros_like(vals_b)
-    diag = diagonal()
-    beam = slots[0]
     pl.semaphore_wait(barrier, 22)
 
     def spread(src, inbox, send, recv, where_to, peers):
@@ -413,24 +425,26 @@
             ref[pl.ds(base + c, 32, stride=8), :] = slots[1 + c] * misfit
 
 
-def misfits(part, resid, slots):
+def gather(take, table, slots, seen_obs):
+    rows = pltpu.VMEM((256, LANES), jnp.float32)
+    block = pltpu.VMEM((16, LANES), jnp.float32)
     return pl.pallas_call(
-        misfit_kernel,
+        gather_kernel,
         out_shape=[f32(256, LANES), f32(256, LANES)],
-        in_specs=[VMEM] * 3,
+        in_specs=[SMEM] + [VMEM] * 3,
         out_specs=[VMEM] * 2,
         scratch_shapes=[
-            pltpu.VMEM((16, LANES), jnp.float32),
+            rows, rows, pltpu.VMEM((STEPS, 32, LANES), jnp.float32), block, block,
             pltpu.VMEM((7, 16, LANES), jnp.float32), pltpu.VMEM((15, 16, LANES), jnp.float32),
             pltpu.SemaphoreType.DMA((7,)), pltpu.SemaphoreType.DMA((7,)),
             pltpu.SemaphoreType.DMA((15,)), pltpu.SemaphoreType.DMA((15,)),
         ],
         compiler_params=pltpu.CompilerParams(collective_id=1, has_side_effects=True, vmem_limit_bytes=16 * MIB),
-        name="misfits",
-    )(part, resid, slots)
-
-
-def scatter_kernel(index, vals_a, vals_b, f3, f2, f1, *sums):
+        name="gather",
+    )(take, table, slots, seen_obs)
+
+
+def scatter_kernel(give, vals_a, vals_b, f3, f2, f1, *sums):
     blank = jnp.zeros((64, LANES), jnp.float32)
 
     def clear(i, carry):
@@ -438,49 +452,49 @@
             ref[pl.ds(pl.multiple_of(i * 64, 64), 64), :] = blank
         return carry
 
-    lax.fori_loop(0, CX * CY * 8 // 64, clear, 0)
+    lax.fori_loop(0, CX * CY * TILE // 64, clear, 0)
     lane8 = lax.broadcasted_iota(jnp.int32, (8, LANES), 1)
-    sum_a, sum_b = sums[:COPIES], sums[COPIES:]
 
     def place(g, carry):
         at = pl.multiple_of(g * 8, 8)
         va = vals_a[pl.ds(at, 8), :]
         vb = vals_b[pl.ds(at, 8), :]
         for j in range(LANES):
-            code = index[g, j]
-            to = pl.ds(pl.multiple_of((code >> 7) * 8, 8), 8)
-            turn = (0 - code) & (LANES - 1)
-            here = lane8 == ((j - code) & (LANES - 1))
-            a, b = sum_a[j % COPIES], sum_b[j % COPIES]
-            a[to, :] = a[to, :] + jnp.where(here, pltpu.roll(va, turn, 1), 0.0)
-            b[to, :] = b[to, :] + jnp.where(here, pltpu.roll(vb, turn, 1), 0.0)
+            code = give[g, j]
+            at = pl.multiple_of(code >> 7, TILE)
+            turn = code & (LANES - 1)
+            here = lane8 == j
+            out = sums[j % COPIES]
+            a, b = pl.ds(at, 8), pl.ds(at + 8, 8)
+            out[a, :] = out[a, :] + pltpu.roll(jnp.where(here, va, 0.0), turn, 1)
+            out[b, :] = out[b, :] + pltpu.roll(jnp.where(here, vb, 0.0), turn, 1)
         return carry
 
     lax.fori_loop(0, 32, place, 0)
 
     def unpack(y, carry):
         for r in range(0, CX, 8):
-            for out, refs, base in ((f3, sum_a, 0), (f2, sum_a, 3), (f1, sum_b, 0)):
+            for out, base in ((f3, 0), (f2, 3), (f1, 8)):
                 for c in range(3):
-                    at = pl.ds((y * CX + r) * 8 + base + c, 8, stride=8)
-                    out[c, y, pl.ds(r, 8), :] = sum(ref[at, :] for ref in refs)
+                    at = pl.ds((y * CX + r) * TILE + base + c, 8, stride=TILE)
+                    out[c, y, pl.ds(r, 8), :] = sum(ref[at, :] for ref in sums)
         return carry
 
     lax.fori_loop(0, CY, unpack, 0)
 
 
-def scatter(index, vals_a, vals_b):
-    table = pltpu.VMEM((CX * CY * 8, LANES), jnp.float32)
+def scatter(give, vals_a, vals_b):
+    table = pltpu.VMEM((CX * CY * TILE, LANES), jnp.float32)
     field = f32(3, CY, CX, LANES)
     return pl.pallas_call(
         scatter_kernel,
         out_shape=[field, field, field],
         in_specs=[SMEM, VMEM, VMEM],
         out_specs=[VMEM] * 3,
-        scratch_shapes=[table] * (2 * COPIES),
+        scratch_shapes=[table] * COPIES,
         compiler_params=pltpu.CompilerParams(vmem_limit_bytes=32 * MIB),
         name="scatter",
-    )(index, vals_a, vals_b)
+    )(give, vals_a, vals_b)
 
 
 def adjoint_kernel(w0, w1, w2, f3, f2, f1, out, a3, a2, a1, sides, inbox, send, recv):
@@ -499,7 +513,19 @@
         return carry
 
     lax.fori_loop(0, CY, fill, 0)
+    clear_rims((a3, a2, a1))
     keep = levels()
+    inside = inside_grid(*where)
+
+    def meet_rims(src, dst, n):
+        for s in range(4):
+            for y in range(0, CY, 8):
+                ref, at = layer_at(src, s, 1, s // 2, y)
+                factor = HALF * (1.0 + ref[at]) if s % 2 else HALF * (1.0 - ref[at])
+                for c in range(3):
+                    v = jnp.where(inside[s], inbox[n, OPPOSITE[s], c, pl.ds(y, 8), :], 0.0)
+                    ref, at = layer_at(dst, s, 0, c, y)
+                    ref[at] = ref[at] + factor * v
 
     def pull(src, adj, dst, force):
         def body(y, r):
@@ -516,11 +542,10 @@
         if n == 0:
             pl.semaphore_wait(barrier, 4)
         copies = send_rims(sides.at[n], inbox.at[n], send.at[n], recv.at[n], *where)
-        over_tile(body, True)
+        over_tile(body)
         for copy in copies:
             copy.wait()
-        unpack_rims(adj, inbox.at[n], *where)
-        over_tile(body, False)
+        meet_rims(src, dst, n)
 
     lane = lax.broadcasted_iota(jnp.int32, (CX, LANES), 1)
     for c in range(3):
@@ -553,12 +578,11 @@
 
 
 def local(initial_state, beam_dir, gate_obs, slot_beam, slot_cell):
-    w0, w1, w2, tab_a, tab_b, index, slots, seen_obs = forward(
+    w0, w1, w2, table, take, give, slots, seen_obs = forward(
         initial_state, slot_cell[0].T, jnp.transpose(gate_obs[:, 0], (0, 2, 1)), slot_beam[0].T, beam_dir
     )
-    resid, part = gather(index, tab_a, tab_b, slots, seen_obs)
-    vals_a, vals_b = misfits(part, resid, slots)
-    fields = scatter(index, vals_a, vals_b)
+    vals_a, vals_b = gather(take, table, slots, seen_obs)
+    fields = scatter(give, vals_a, vals_b)
     return adjoint((w0, w1, w2), fields)
 
 

time: 111 us -> 89.1 us (0.80)
  Pallas kernels: 105 us -> 83.5 us
    pallas_call x3 -> x2, Pallas kernels: 60 us -> 48.9 us  [the longest x1 26.8 us: forward(): pl.pallas_call(forward_kernel, out_shape=[wide, wide, wide, table, codes,...]
    pallas_call x1, Pallas kernels: 27.6 us -> 17.1 us  [adjoint(): pl.pallas_call(adjoint_kernel, out_shape=f32(3, CX, CY * NZ), in_specs=[V...]
where the time goes in v1:
time: 89.1 us; the launch traced here: 88.7 us
  Pallas kernels  83.5 us (94%)
  local copies, waits for them, and re-layouts  5.2 us (6%)
    pallas_call x1, Pallas kernels, forward(): pl.pallas_call(forward_kernel, out_shape=[wide, wide, wide, table, codes,...  26.8 us
    pallas_call x1, Pallas kernels, gather(): pl.pallas_call(gather_kernel, out_shape=[f32(256, LANES), f32(256, LANES)...  22.2 us
    pallas_call x1, Pallas kernels, scatter(): pl.pallas_call(scatter_kernel, out_shape=[field, field, field], in_specs=...  17.4 us
    pallas_call x1, Pallas kernels, adjoint(): pl.pallas_call(adjoint_kernel, out_shape=f32(3, CX, CY * NZ), in_specs=[V...  17.1 us
    unnamed x11, local copies, waits for them, and re-layouts  5.2 us

profile of v1, /device:TPU:0, one launch (start us, length us, event | category | flops | bytes accessed | tf_op | source)
XLA Modules:
  0.0 88.7 jit_solution(16022279073927216500)
XLA Ops:
  0.0 0.0 copy-start
  0.0 1.3 %copy-done = f32[3,32,3072]{2,1,0:T(8,128)S(1)} copy-done((f32[3,32,3072]{2,1,0:T(8,128)S(1)}, f32[3,32,3072]{2,1,0:T(8,128)}, u32[]{:S(2)}) %copy-start) | copy-done | bytes 1179672
  1.3 0.0 copy-start.1
  1.3 0.8 copy-done.1
  2.1 0.0 copy-start.2
  2.1 0.7 copy-done.2
  2.8 0.0 copy-start.3
  2.8 0.7 copy-done.3
  3.5 0.0 copy-start.4
  3.5 0.7 copy-done.4
  4.2 26.8 %forward.1 = (f32[3,34,48,128]{3,2,1,0:T(8,128)S(1)}, f32[3,34,48,128]{3,2,1,0:T(8,128)S(1)}, f32[3,34,48,128]{3,2,1,0:T(8,128)S(1)}, f32[1024,16,128]{2,1,0:T(8...) custom-call(f32[3,32,3072]{2,1,0:T(8,128)S(1)} %copy-done, ...), custom_call_target="tpu_custom_call" | custom-call | tf_op jit(solution)/shard_map/forward/pallas_call | solution.py:299
  31.0 22.2 %gather.1 = (f32[256,128]{1,0:T(8,128)S(1)}, f32[256,128]{1,0:T(8,128)S(1)}) custom-call(s32[32,128]{1,0:T(8,128)S(1)} %get-tuple-element.22.take, f32[1024,16,128]{2,1,0:T(8,128)S(1)} %get-tuple-element.23.table, f32[4,32,128]{2,1,0:T(8,128)S(1)} %get-tuple-element.24.slots, f32[3,32,128]{2,1,0:T(8,128)S(1)} %get-tuple-element.25.seen_obs), custom_call_target="tpu_custom_call" | custom-call | tf_op jit(solution)/shard_map/gather/pallas_call | solution.py:431
  53.1 17.4 %scatter.1 = (f32[3,32,32,128]{3,2,1,0:T(8,128)S(1)}, f32[3,32,32,128]{3,2,1,0:T(8,128)S(1)}, f32[3,32,32,128]{3,2,1,0:T(8,128)S(1)}) custom-call(s32[32,128]{1,0:T(8,128)S(1)} %get-tuple-element.21.give, f32[256,128]{1,0:T(8,128)S(1)} %get-tuple-element.26.vals_a, f32[256,128]{1,0:T(8,128)S(1)} %get-tuple-element.27.vals_b), custom_call_target="tpu_custom_call" | custom-call | tf_op jit(solution)/shard_map/scatter/pallas_call | solution.py:489
  70.6 17.1 %adjoint.1 = f32[3,32,3072]{2,1,0:T(8,128)S(1)} custom-call(f32[3,34,48,128]{3,2,1,0:T(8,128)S(1)} %get-tuple-element.18.w0, f32[3,34,48,128]{3,2,1,0:T(8,128)S(1)} %get-tuple-element.19.w1, f32[3,34,48,128]{3,2,1,0:T(8,128)S(1)} %get-tuple-element.20.w2, f32[3,32,32,128]{3,2,1,0:T(8,128)S(1)} %get-tuple-element.28.f3, ...), custom_call_target="tpu_custom_call" | custom-call | tf_op jit(solution)/shard_map/adjoint/pallas_call | solution.py:567
  87.7 1.0 %copy.7 = f32[3,32,3072]{2,1,0:T(8,128)} copy(f32[3,32,3072]{2,1,0:T(8,128)S(1)} %adjoint.1) | data formatting | bytes 2359296
Async XLA Ops:
  0.0 1.3 %copy-start = (f32[3,32,3072]{2,1,0:T(8,128)S(1)}, f32[3,32,3072]{2,1,0:T(8,128)}, u32[]{:S(2)}) copy-start(f32[3,32,3072]{2,1,0:T(8,128)} %state.1) | copy-start | bytes 3538948
  1.3 0.8 copy-start.1
  2.1 0.7 copy-start.2
  2.8 0.7 copy-start.3
  3.5 0.7 copy-start.4

commit v2 on v1

--- a/solution.py
+++ b/solution.py
@@ -18,8 +18,8 @@
 TOP = 8
 ROWS = CX + 2 * TOP
 WIDE = CY + 2
-COPIES = 2
-TILE = 16
+COPIES = 3
+TILE = 8
 UNROLL = 4
 MIB = 1024 * 1024
 MESH = pl.DeviceIdType.MESH
@@ -161,8 +161,8 @@
 
 
 def forward_kernel(
-    state, cell, obs, beam, beam_dir,
-    w0, w1, w2, table, take, give, slots, seen_obs,
+    state, lists,
+    w0, w1, w2, table, take, give, third, slots, seen_obs,
     got, msg, sides, inbox, send, recv, list_send, list_recv, own,
 ):
     n_gx, n_gy, gx, gy = sizes()
@@ -179,15 +179,15 @@
         return carry
 
     lax.fori_loop(1, count, hail, 0)
-    kind = beam[...]
-    heads = [cell[...].astype(jnp.float32), obs[0], obs[1], obs[2]]
-    tails = [kind.astype(jnp.float32)]
+    kind = lists[pl.ds(LANES, 32), :]
+    tails = [kind]
+    beam_dir = lists[pl.ds(LANES + 32, 8), :]
     for c in range(3):
         weight = jnp.zeros(kind.shape, jnp.float32)
         for b in range(BEAMS):
-            weight = jnp.where(kind == b, beam_dir[c, b], weight)
+            weight = jnp.where(kind == float(b), beam_dir[c : c + 1, b : b + 1], weight)
         tails.append(weight)
-    msg[:, 0, :] = jnp.concatenate(heads, axis=0).T
+    msg[:, 0, :] = lists[pl.ds(0, LANES), :].T
     msg[:, 1, :] = jnp.concatenate(tails, axis=0).T
 
     lane = lax.broadcasted_iota(jnp.int32, (CX, LANES), 1)
@@ -233,10 +233,12 @@
 
     def tables(y, r):
         at = ((y - 1) * CX + (r - TOP)) * TILE
+        spare = w1[2, y, pl.ds(r, 8), :]
         for c, v in enumerate(step_block(w2, y, r)):
-            cells[pl.ds(at + c, 8, stride=TILE), :] = v
+            cells[pl.ds(at + c, 8, stride=TILE), :] = jnp.where(keep, v, pltpu.roll(spare, NZ - 32 * c, 1))
             cells[pl.ds(at + 3 + c, 8, stride=TILE), :] = w2[c, y, pl.ds(r, 8), :]
-            cells[pl.ds(at + 8 + c, 8, stride=TILE), :] = w1[c, y, pl.ds(r, 8), :]
+            if c < 2:
+                cells[pl.ds(at + 6 + c, 8, stride=TILE), :] = w1[c, y, pl.ds(r, 8), :]
 
     def target(dst, s, c, y):
         if dst is not None:
@@ -282,25 +284,28 @@
     y = ((rem >> 5) * 171) >> 9
     z = rem - y * NZ
     lane = lax.broadcasted_iota(jnp.int32, (32, LANES), 1)
-    at = (y * CX + x) * (TILE * LANES)
+    at = (y * CX + x) * LANES
     take[...] = at + ((lane - z) & (LANES - 1))
-    give[...] = at + ((z - lane) & (LANES - 1))
+    give[...] = at * TILE + ((z - lane) & (LANES - 1))
+    third[...] = (z >> 5).astype(jnp.float32)
     for j in range(4):
         slots[j] = regroup(g1, j)
     for n in range(STEPS):
         seen_obs[n] = regroup(g0, 1 + n)
 
 
-def forward(state, cell, obs, beam, beam_dir):
-    count = cell.shape[1]
+def forward(state, lists):
+    count = lists.shape[1]
     wide, table = f32(3, WIDE, ROWS, LANES), f32(CX * CY, TILE, LANES)
     codes = jax.ShapeDtypeStruct((32, LANES), jnp.int32)
     rim = pltpu.VMEM((STEPS, 4, 3, 32, LANES), jnp.float32)
     return pl.pallas_call(
         forward_kernel,
-        out_shape=[wide, wide, wide, table, codes, codes, f32(4, 32, LANES), f32(STEPS, 32, LANES)],
-        in_specs=[VMEM] * 4 + [SMEM],
-        out_specs=[VMEM] * 8,
+        out_shape=[
+            wide, wide, wide, table, codes, codes, f32(32, LANES), f32(4, 32, LANES), f32(STEPS, 32, LANES),
+        ],
+        in_specs=[VMEM] * 2,
+        out_specs=[VMEM] * 9,
         scratch_shapes=[
             pltpu.VMEM((count, 2, LANES), jnp.float32), pltpu.VMEM((count, 2, LANES), jnp.float32), rim, rim,
             pltpu.SemaphoreType.DMA((STEPS, 4)), pltpu.SemaphoreType.DMA((STEPS, 4)),
@@ -308,7 +313,13 @@
         ],
         compiler_params=pltpu.CompilerParams(collective_id=0, has_side_effects=True, vmem_limit_bytes=24 * MIB),
         name="forward",
-    )(state, cell, obs, beam, beam_dir)
+    )(state, lists)
+
+
+def spare_lanes():
+    lane = lax.broadcasted_iota(jnp.int32, (8, LANES), 1)
+    row = lax.broadcasted_iota(jnp.int32, (8, LANES), 0)
+    return jnp.where(row < 3, (lane + 32 * (row + 1)) & (LANES - 1), -1)
 
 
 def same_list():
@@ -331,8 +342,15 @@
 
 
 def gather_kernel(
-    take, table, slots, seen_obs,
-    vals_a, vals_b,
+    take, table, third, slots, seen_obs,
+    vals_a, vals_b, *rest,
+):
+    empty = rest[:COPIES]
+    gather_body(take, table, third, slots, seen_obs, vals_a, vals_b, empty, *rest[COPIES:])
+
+
+def gather_body(
+    take, table, third, slots, seen_obs, vals_a, vals_b, empty,
     acc_a, acc_b, resid, part, half, inbox_a, inbox_b, send_a, recv_a, send_b, recv_b,
 ):
     gx, gy = lax.axis_index("gx"), lax.axis_index("gy")
@@ -358,16 +376,16 @@
     part[...] = jnp.zeros_like(part)
 
     lane8 = lax.broadcasted_iota(jnp.int32, (8, LANES), 1)
+    spare = spare_lanes()
 
     def pick(g, carry):
         a = jnp.zeros((8, LANES), jnp.float32)
         b = jnp.zeros((8, LANES), jnp.float32)
         for j in range(LANES):
             code = take[g, j]
-            tile = pltpu.roll(table[code >> 11], code & (LANES - 1), 1)
-            here = lane8 == j
-            a = jnp.where(here, tile[:8], a)
-            b = jnp.where(here, tile[8:], b)
+            tile = pltpu.roll(table[code >> 7], code & (LANES - 1), 1)
+            a = jnp.where(lane8 == j, tile, a)
+            b = jnp.where(spare == j, tile, b)
         at = pl.multiple_of(g * 8, 8)
         acc_a[pl.ds(at, 8), :] = a
         acc_b[pl.ds(at, 8), :] = b
@@ -379,8 +397,15 @@
     beam = slots[0]
     values = []
     for n in range(STEPS):
-        ref, base = ((acc_b, 0), (acc_a, 3), (acc_a, 0))[n]
-        seen = sum(slots[1 + c] * ref[pl.ds(base + c, 32, stride=8), :] for c in range(3))
+        base = (6, 3, 0)[n]
+        got = [acc_a[pl.ds(base + c, 32, stride=8), :] for c in range(3 if n else 2)]
+        if n == 0:
+            ninth = jnp.zeros((32, LANES), jnp.float32)
+            for k in range(3):
+                piece = pltpu.roll(acc_b[pl.ds(k, 32, stride=8), :], 32 * (k + 1), 1)
+                ninth = jnp.where(third[...] == float(k), piece, ninth)
+            got.append(ninth)
+        seen = sum(slots[1 + c] * got[c] for c in range(3))
         r = seen - seen_obs[n]
         resid[n] = r
         for b in range(BEAMS):
@@ -391,7 +416,16 @@
         part[pl.ds(i, 1), :] = jnp.sum(block, axis=0, keepdims=True)
     pl.semaphore_wait(barrier, 22)
 
-    def spread(src, inbox, send, recv, where_to, peers):
+    blank = jnp.zeros((64, LANES), jnp.float32)
+
+    def clear(i, carry):
+        for ref in empty:
+            ref[pl.ds(pl.multiple_of(i * 64, 64), 64), :] = blank
+        return carry
+
+    half_way = CX * CY * TILE // 128
+
+    def spread(src, inbox, send, recv, where_to, peers, first):
         copies = []
         for d in range(1, peers):
             copy = pltpu.make_async_remote_copy(
@@ -400,15 +434,16 @@
             )
             copy.start()
             copies.append(copy)
+        lax.fori_loop(first, first + half_way, clear, 0)
         for copy in copies:
             copy.wait()
 
-    spread(part, inbox_a, send_a, recv_a, near, 8)
+    spread(part, inbox_a, send_a, recv_a, near, 8, 0)
     acc = part[...]
     for d in range(7):
         acc = acc + inbox_a[d]
     half[...] = acc
-    spread(half, inbox_b, send_b, recv_b, far, 16)
+    spread(half, inbox_b, send_b, recv_b, far, 16, half_way)
     for d in range(15):
         acc = acc + inbox_b[d]
 
@@ -420,19 +455,24 @@
         for b in range(BEAMS):
             mean = jnp.where(beam == float(b), means[at + 32 * b : at + 32 * b + 32, :], mean)
         misfit = jnp.where(beam >= 0.0, resid[n] - mean, 0.0)
-        ref, base = ((vals_b, 0), (vals_a, 3), (vals_a, 0))[n]
+        base = (6, 3, 0)[n]
         for c in range(3):
-            ref[pl.ds(base + c, 32, stride=8), :] = slots[1 + c] * misfit
-
-
-def gather(take, table, slots, seen_obs):
+            if base + c < 8:
+                vals_a[pl.ds(base + c, 32, stride=8), :] = slots[1 + c] * misfit
+                continue
+            for k in range(3):
+                piece = jnp.where(third[...] == float(k), slots[1 + c] * misfit, 0.0)
+                vals_b[pl.ds(k, 32, stride=8), :] = pltpu.roll(piece, NZ - 32 * k, 1)
+
+
+def gather(take, table, third, slots, seen_obs):
     rows = pltpu.VMEM((256, LANES), jnp.float32)
     block = pltpu.VMEM((16, LANES), jnp.float32)
     return pl.pallas_call(
         gather_kernel,
-        out_shape=[f32(256, LANES), f32(256, LANES)],
-        in_specs=[SMEM] + [VMEM] * 3,
-        out_specs=[VMEM] * 2,
+        out_shape=[f32(256, LANES), f32(256, LANES)] + [f32(CX * CY * TILE, LANES)] * COPIES,
+        in_specs=[SMEM] + [VMEM] * 4,
+        out_specs=[VMEM] * (2 + COPIES),
         scratch_shapes=[
             rows, rows, pltpu.VMEM((STEPS, 32, LANES), jnp.float32), block, block,
             pltpu.VMEM((7, 16, LANES), jnp.float32), pltpu.VMEM((15, 16, LANES), jnp.float32),
@@ -441,19 +481,14 @@
         ],
         compiler_params=pltpu.CompilerParams(collective_id=1, has_side_effects=True, vmem_limit_bytes=16 * MIB),
         name="gather",
-    )(take, table, slots, seen_obs)
-
-
-def scatter_kernel(give, vals_a, vals_b, f3, f2, f1, *sums):
-    blank = jnp.zeros((64, LANES), jnp.float32)
-
-    def clear(i, carry):
-        for ref in sums:
-            ref[pl.ds(pl.multiple_of(i * 64, 64), 64), :] = blank
-        return carry
-
-    lax.fori_loop(0, CX * CY * TILE // 64, clear, 0)
+    )(take, table, third, slots, seen_obs)
+
+
+def scatter_kernel(give, vals_a, vals_b, *rest):
+    f3, f2, f1 = rest[COPIES : COPIES + 3]
+    sums = rest[COPIES + 3 :]
     lane8 = lax.broadcasted_iota(jnp.int32, (8, LANES), 1)
+    spare = spare_lanes()
 
     def place(g, carry):
         at = pl.multiple_of(g * 8, 8)
@@ -461,40 +496,44 @@
         vb = vals_b[pl.ds(at, 8), :]
         for j in range(LANES):
             code = give[g, j]
-            at = pl.multiple_of(code >> 7, TILE)
-            turn = code & (LANES - 1)
-            here = lane8 == j
+            to = pl.ds(pl.multiple_of(code >> 7, TILE), TILE)
+            v = jnp.where(lane8 == j, va, jnp.where(spare == j, vb, 0.0))
             out = sums[j % COPIES]
-            a, b = pl.ds(at, 8), pl.ds(at + 8, 8)
-            out[a, :] = out[a, :] + pltpu.roll(jnp.where(here, va, 0.0), turn, 1)
-            out[b, :] = out[b, :] + pltpu.roll(jnp.where(here, vb, 0.0), turn, 1)
+            out[to, :] = out[to, :] + pltpu.roll(v, code & (LANES - 1), 1)
         return carry
 
     lax.fori_loop(0, 32, place, 0)
+    keep = lane8 < NZ
 
     def unpack(y, carry):
         for r in range(0, CX, 8):
-            for out, base in ((f3, 0), (f2, 3), (f1, 8)):
+            rows = []
+            for k in range(8):
+                at = pl.ds((y * CX + r) * TILE + k, 8, stride=TILE)
+                rows.append(sum(ref[at, :] for ref in sums))
+            pieces = [pltpu.roll(rows[k], 32 * (k + 1), 1) for k in range(3)]
+            ninth = jnp.where(lane8 < 32, pieces[0], jnp.where(lane8 < 64, pieces[1], pieces[2]))
+            rows = [jnp.where(keep, v, 0.0) for v in rows[:3]] + rows[3:] + [jnp.where(keep, ninth, 0.0)]
+            for i, out in enumerate((f3, f2, f1)):
                 for c in range(3):
-                    at = pl.ds((y * CX + r) * TILE + base + c, 8, stride=TILE)
-                    out[c, y, pl.ds(r, 8), :] = sum(ref[at, :] for ref in sums)
+                    out[c, y, pl.ds(r, 8), :] = rows[3 * i + c]
         return carry
 
     lax.fori_loop(0, CY, unpack, 0)
 
 
-def scatter(give, vals_a, vals_b):
-    table = pltpu.VMEM((CX * CY * TILE, LANES), jnp.float32)
+def scatter(give, vals_a, vals_b, empty):
+    table = f32(CX * CY * TILE, LANES)
     field = f32(3, CY, CX, LANES)
     return pl.pallas_call(
         scatter_kernel,
-        out_shape=[field, field, field],
-        in_specs=[SMEM, VMEM, VMEM],
-        out_specs=[VMEM] * 3,
-        scratch_shapes=[table] * COPIES,
-        compiler_params=pltpu.CompilerParams(vmem_limit_bytes=32 * MIB),
+        out_shape=[field, field, field] + [table] * COPIES,
+        in_specs=[SMEM] + [VMEM] * (2 + COPIES),
+        out_specs=[VMEM] * (3 + COPIES),
+        input_output_aliases={3 + i: 3 + i for i in range(COPIES)},
+        compiler_params=pltpu.CompilerParams(vmem_limit_bytes=16 * MIB),
         name="scatter",
-    )(give, vals_a, vals_b)
+    )(give, vals_a, vals_b, *empty)[:3]
 
 
 def adjoint_kernel(w0, w1, w2, f3, f2, f1, out, a3, a2, a1, sides, inbox, send, recv):
@@ -578,11 +617,22 @@
 
 
 def local(initial_state, beam_dir, gate_obs, slot_beam, slot_cell):
-    w0, w1, w2, table, take, give, slots, seen_obs = forward(
-        initial_state, slot_cell[0].T, jnp.transpose(gate_obs[:, 0], (0, 2, 1)), slot_beam[0].T, beam_dir
+    count = slot_cell.shape[1]
+    capacity = slot_cell.shape[2]
+    rows = 5 * capacity + 8
+
+    def at_row(block, first):
+        return jnp.pad(block, ((first, rows - first - block.shape[0]), (0, count - block.shape[1])))
+
+    lists = (
+        at_row(slot_cell[0].T.astype(jnp.float32), 0)
+        + at_row(jnp.transpose(gate_obs[:, 0], (0, 2, 1)).reshape(-1, count), capacity)
+        + at_row(slot_beam[0].T.astype(jnp.float32), 4 * capacity)
+        + at_row(beam_dir, 5 * capacity)
     )
-    vals_a, vals_b = gather(take, table, slots, seen_obs)
-    fields = scatter(give, vals_a, vals_b)
+    w0, w1, w2, table, take, give, third, slots, seen_obs = forward(initial_state, lists)
+    vals_a, vals_b, *empty = gather(take, table, third, slots, seen_obs)
+    fields = scatter(give, vals_a, vals_b, empty)
     return adjoint((w0, w1, w2), fields)
 
 

time: 89.1 us -> 81.4 us (0.914)
  Pallas kernels: 83.5 us -> 77.3 us
  local copies, waits for them, and re-layouts: 5.2 us -> 2.28 us
  other arithmetic: 0 us -> 1.56 us
    pallas_call x1, Pallas kernels: 17.4 us -> 14.2 us  [scatter(): pl.pallas_call(scatter_kernel, out_shape=[field, field, field] + [table]...]
    unnamed x11 -> x3, local copies, waits for them, and re-layouts: 5.2 us -> 2.28 us
    pallas_call x1, Pallas kernels: 22.2 us -> 20.2 us  [gather(): pl.pallas_call(gather_kernel, out_shape=[f32(256, LANES), f32(256, LANES)...]
    pallas_call x1, Pallas kernels: 26.8 us -> 25.8 us  [forward(): pl.pallas_call(forward_kernel, out_shape=[wide, wide, wide, table, codes,...]
where the time goes in v2:
time: 81.4 us; the launch traced here: 81.2 us
  Pallas kernels  77.3 us (95%)
  local copies, waits for them, and re-layouts  2.28 us (3%)
  other arithmetic  1.56 us (2%)
    pallas_call x1, Pallas kernels, forward(): pl.pallas_call(forward_kernel, out_shape=[wide, wide, wide, table, codes,...  25.8 us
    pallas_call x1, Pallas kernels, gather(): pl.pallas_call(gather_kernel, out_shape=[f32(256, LANES), f32(256, LANES)...  20.2 us
    pallas_call x1, Pallas kernels, adjoint(): pl.pallas_call(adjoint_kernel, out_shape=f32(3, CX, CY * NZ), in_specs=[V...  17.1 us
    pallas_call x1, Pallas kernels, scatter(): pl.pallas_call(scatter_kernel, out_shape=[field, field, field] + [table]...  14.2 us
    unnamed x3, local copies, waits for them, and re-layouts  2.28 us

profile of v2, /device:TPU:0, one launch (start us, length us, event | category | flops | bytes accessed | tf_op | source)
XLA Modules:
  0.0 81.2 jit_solution(13606560478676979157)
XLA Ops:
  0.0 0.7 convert_bitcast_fusion
  0.7 0.8 %pad_add_fusion.lists = f32[168,128]{1,0:T(8,128)S(1)} fusion(f32[3,4]{1,0:T(4,128)} %param.6, f32[32,128]{1,0:T(8,128)S(1)} %get-tuple-element.39, f32[96,128]{1,0:T(8,128)} %bitcast.13, f32[32,128]{1,0:T(8,128)S(1)} %get-tuple-element.40), kind=kLoop, calls=%fused_computation | loop fusion | flops 64512 | bytes 167984 | tf_op jit(solution)/shard_map/add | solution.py:628
  1.6 0.0 copy-start
  1.6 1.3 %copy-done = f32[3,32,3072]{2,1,0:T(8,128)S(1)} copy-done((f32[3,32,3072]{2,1,0:T(8,128)S(1)}, f32[3,32,3072]{2,1,0:T(8,128)}, u32[]{:S(2)}) %copy-start) | copy-done | bytes 1179672
  2.8 25.8 %forward.1 = (f32[3,34,48,128]{3,2,1,0:T(8,128)S(1)}, f32[3,34,48,128]{3,2,1,0:T(8,128)S(1)}, f32[3,34,48,128]{3,2,1,0:T(8,128)S(1)}, f32[1024,8,128]{2,1,0:T(8,...) custom-call(f32[3,32,3072]{2,1,0:T(8,128)S(1)} %copy-done, ...), custom_call_target="tpu_custom_call" | custom-call | tf_op jit(solution)/shard_map/forward/pallas_call | solution.py:302
  28.7 20.2 %gather.1 = (f32[256,128]{1,0:T(8,128)S(1)}, f32[256,128]{1,0:T(8,128)S(1)}, f32[8192,128]{1,0:T(8,128)S(1)}, f32[8192,128]{1,0:T(8,128)S(1)}, f32[8192,128]{1,0:T(8,128)S(1)}) custom-call(s32[32,128]{1,0:T(8,128)S(1)} %get-tuple-element.26.take, f32[1024,8,128]{2,1,0:T(8,128)S(1)} %get-tuple-element.27.table, f32[32,128]{1,0:T(8,128)S(1)} %get-tuple-element.28.third, ...), custom_call_target="tpu_custom_call" | custom-call | tf_op jit(solution)/shard_map/gather/pallas_call | solution.py:471
  48.9 14.2 %scatter.1 = (f32[3,32,32,128]{3,2,1,0:T(8,128)S(1)}, f32[3,32,32,128]{3,2,1,0:T(8,128)S(1)}, f32[3,32,32,128]{3,2,1,0:T(8,128)S(1)}, f32[8192,128]{1,0:T(8,128)...) custom-call(s32[32,128]{1,0:T(8,128)S(1)} %get-tuple-element.25.give, ...), custom_call_target="tpu_custom_call", output_to_operand_aliasing={{3}: (3, {}), {4}: (4, {}), {5}: (5, {})} | custom-call | tf_op jit(solution)/shard_map/scatter/pallas_call | solution.py:528
  63.0 17.1 %adjoint.1 = f32[3,32,3072]{2,1,0:T(8,128)S(1)} custom-call(f32[3,34,48,128]{3,2,1,0:T(8,128)S(1)} %get-tuple-element.22.w0, f32[3,34,48,128]{3,2,1,0:T(8,128)S(1)} %get-tuple-element.23.w1, f32[3,34,48,128]{3,2,1,0:T(8,128)S(1)} %get-tuple-element.24.w2, f32[3,32,32,128]{3,2,1,0:T(8,128)S(1)} %get-tuple-element.36.f3, ...), custom_call_target="tpu_custom_call" | custom-call | tf_op jit(solution)/shard_map/adjoint/pallas_call | solution.py:606
  80.2 1.0 %copy.13 = f32[3,32,3072]{2,1,0:T(8,128)} copy(f32[3,32,3072]{2,1,0:T(8,128)S(1)} %adjoint.1) | data formatting | bytes 2359296
Async XLA Ops:
  1.6 1.3 %copy-start = (f32[3,32,3072]{2,1,0:T(8,128)S(1)}, f32[3,32,3072]{2,1,0:T(8,128)}, u32[]{:S(2)}) copy-start(f32[3,32,3072]{2,1,0:T(8,128)} %state.1) | copy-start | bytes 3538948

commit v3 on v2

--- a/solution.py
+++ b/solution.py
@@ -18,7 +18,7 @@
 TOP = 8
 ROWS = CX + 2 * TOP
 WIDE = CY + 2
-COPIES = 3
+COPIES = 4
 TILE = 8
 UNROLL = 4
 MIB = 1024 * 1024
@@ -89,7 +89,8 @@
         (gx, lax.rem(gy + n_gy - 1, n_gy)), (gx, lax.rem(gy + 1, n_gy)),
     )
     copies = []
-    for s, target in enumerate(targets):
+    for s in (2, 3, 0, 1):
+        target = targets[s]
         copy = pltpu.make_async_remote_copy(
             src_ref=sides.at[s], dst_ref=inbox.at[s], send_sem=send.at[s], recv_sem=recv.at[s],
             device_id=target, device_id_type=MESH,
@@ -163,33 +164,27 @@
 def forward_kernel(
     state, lists,
     w0, w1, w2, table, take, give, third, slots, seen_obs,
-    got, msg, sides, inbox, send, recv, list_send, list_recv, own,
+    got, mid, msg, sides, inbox, send, recv, list_send, list_recv, own,
 ):
     n_gx, n_gy, gx, gy = sizes()
-    count = n_gx * n_gy
-    me = gx * n_gy + gy
     barrier = pltpu.get_barrier_semaphore()
 
-    def device(i):
-        peer = lax.rem(me + i, count)
-        return peer, (peer // n_gy, lax.rem(peer, n_gy))
-
-    def hail(i, carry):
-        pl.semaphore_signal(barrier, inc=1, device_id=device(i)[1], device_id_type=MESH)
-        return carry
-
-    lax.fori_loop(1, count, hail, 0)
-    kind = lists[pl.ds(LANES, 32), :]
-    tails = [kind]
-    beam_dir = lists[pl.ds(LANES + 32, 8), :]
-    for c in range(3):
-        weight = jnp.zeros(kind.shape, jnp.float32)
-        for b in range(BEAMS):
-            weight = jnp.where(kind == float(b), beam_dir[c : c + 1, b : b + 1], weight)
-        tails.append(weight)
-    msg[:, 0, :] = lists[pl.ds(0, LANES), :].T
-    msg[:, 1, :] = jnp.concatenate(tails, axis=0).T
-
+    def along_x(i):
+        to = lax.rem(gx + i, n_gx)
+        return to, (to, gy)
+
+    def along_y(i):
+        to = lax.rem(gy + i, n_gy)
+        return to, (gx, to)
+
+    def hail(line):
+        def body(i, carry):
+            pl.semaphore_signal(barrier, inc=1, device_id=line(i)[1], device_id_type=MESH)
+            return carry
+        return body
+
+    lax.fori_loop(1, n_gx, hail(along_x), 0)
+    lax.fori_loop(1, n_gy, hail(along_y), 0)
     lane = lax.broadcasted_iota(jnp.int32, (CX, LANES), 1)
     for c in range(3):
         for y in range(0, CY, 4):
@@ -203,24 +198,52 @@
             for i, v in enumerate(planes):
                 w0[c, y + 1 + i, pl.ds(TOP, CX), :] = jnp.where(lane < NZ, v, 0.0)
     pack_rims(w0, sides.at[0])
-    clear_rims((w0, w1, w2))
-    pl.semaphore_wait(barrier, count - 1)
+    pl.semaphore_wait(barrier, n_gx + n_gy - 2)
 
     where = (n_gx, n_gy, gx, gy)
     copies = send_rims(sides.at[0], inbox.at[0], send.at[0], recv.at[0], *where)
-
-    def post(i, carry):
-        peer, target = device(i)
+    kind = lists[pl.ds(LANES, 32), :]
+    tails = [kind]
+    beam_dir = lists[pl.ds(LANES + 32, 8), :]
+    for c in range(3):
+        weight = jnp.zeros(kind.shape, jnp.float32)
+        for b in range(BEAMS):
+            weight = jnp.where(kind == float(b), beam_dir[c : c + 1, b : b + 1], weight)
+        tails.append(weight)
+    msg[:, :, 0, :] = lists[pl.ds(0, LANES), :].T.reshape(n_gx, n_gy, LANES)
+    msg[:, :, 1, :] = jnp.concatenate(tails, axis=0).T.reshape(n_gx, n_gy, LANES)
+
+
+    def post(src, dst, line, sems):
+        def body(i, carry):
+            to, target = line(i)
+            pltpu.make_async_remote_copy(
+                src_ref=src(to), dst_ref=dst, send_sem=list_send.at[sems], recv_sem=list_recv.at[sems],
+                device_id=target, device_id_type=MESH,
+            ).start()
+            return carry
+        return body
+
+    def settle(src, dst, line, sems):
         pltpu.make_async_remote_copy(
-            src_ref=msg.at[peer], dst_ref=got.at[me], send_sem=list_send, recv_sem=list_recv,
-            device_id=target, device_id_type=MESH,
-        ).start()
-        return carry
-
-    lax.fori_loop(1, count, post, 0)
-    mine = pltpu.make_async_copy(msg.at[me], got.at[me], own)
+            src_ref=src, dst_ref=dst, send_sem=list_send.at[sems], recv_sem=list_recv.at[sems],
+            device_id=line(1)[1], device_id_type=MESH,
+        ).wait()
+
+    lax.fori_loop(1, n_gx, post(lambda to: msg.at[to], mid.at[gx], along_x, 0), 0)
+    mine = pltpu.make_async_copy(msg.at[gx], mid.at[gx], own.at[0])
     mine.start()
 
+    def forward_lists():
+        mine.wait()
+        rest = pl.ds(0, n_gx - 1)
+        settle(msg.at[rest], mid.at[rest], along_x, 0)
+        lax.fori_loop(1, n_gy, post(lambda to: mid.at[:, to], got.at[:, gy], along_y, 1), 0)
+        copy = pltpu.make_async_copy(mid.at[:, gy], got.at[:, gy], own.at[1])
+        copy.start()
+        return copy
+
+    clear_rims((w0, w1, w2))
     keep = levels()
 
     def advance(src, dst):
@@ -266,18 +289,18 @@
         if n:
             pack_rims(src, sides.at[n])
             copies = send_rims(sides.at[n], inbox.at[n], send.at[n], recv.at[n], *where)
+        if n == 1:
+            last = forward_lists()
         over_tile(body)
         for copy in copies:
             copy.wait()
         meet_rims(src, dst, n)
 
-    mine.wait()
-    rest = pl.ds(0, count - 1)
-    pltpu.make_async_remote_copy(
-        src_ref=msg.at[rest], dst_ref=got.at[rest], send_sem=list_send, recv_sem=list_recv,
-        device_id=device(1)[1], device_id_type=MESH,
-    ).wait()
-    g0, g1 = got[:, 0, :], got[:, 1, :]
+    last.wait()
+    rest = pl.ds(0, n_gy - 1)
+    settle(mid.at[:, rest], got.at[:, rest], along_y, 1)
+    g0 = got[:, :, 0, :].reshape(LANES, LANES)
+    g1 = got[:, :, 1, :].reshape(LANES, LANES)
     where_to = regroup(g0, 0).astype(jnp.int32)
     x = ((where_to >> 10) * 171) >> 9
     rem = where_to - x * (CY * NZ)
@@ -295,7 +318,7 @@
 
 
 def forward(state, lists):
-    count = lists.shape[1]
+    box = pltpu.VMEM((lax.axis_size("gx"), lax.axis_size("gy"), 2, LANES), jnp.float32)
     wide, table = f32(3, WIDE, ROWS, LANES), f32(CX * CY, TILE, LANES)
     codes = jax.ShapeDtypeStruct((32, LANES), jnp.int32)
     rim = pltpu.VMEM((STEPS, 4, 3, 32, LANES), jnp.float32)
@@ -307,9 +330,9 @@
         in_specs=[VMEM] * 2,
         out_specs=[VMEM] * 9,
         scratch_shapes=[
-            pltpu.VMEM((count, 2, LANES), jnp.float32), pltpu.VMEM((count, 2, LANES), jnp.float32), rim, rim,
+            box, box, box, rim, rim,
             pltpu.SemaphoreType.DMA((STEPS, 4)), pltpu.SemaphoreType.DMA((STEPS, 4)),
-            pltpu.SemaphoreType.DMA, pltpu.SemaphoreType.DMA, pltpu.SemaphoreType.DMA,
+            pltpu.SemaphoreType.DMA((2,)), pltpu.SemaphoreType.DMA((2,)), pltpu.SemaphoreType.DMA((2,)),
         ],
         compiler_params=pltpu.CompilerParams(collective_id=0, has_side_effects=True, vmem_limit_bytes=24 * MIB),
         name="forward",
@@ -391,7 +414,7 @@
         acc_b[pl.ds(at, 8), :] = b
         return carry
 
-    lax.fori_loop(0, 32, pick, 0)
+    lax.fori_loop(0, 32, pick, 0, unroll=4)
 
     diag = diagonal()
     beam = slots[0]
@@ -486,7 +509,8 @@
 
 def scatter_kernel(give, vals_a, vals_b, *rest):
     f3, f2, f1 = rest[COPIES : COPIES + 3]
-    sums = rest[COPIES + 3 :]
+    sums = rest[COPIES + 3 : -1]
+    layer = rest[-1]
     lane8 = lax.broadcasted_iota(jnp.int32, (8, LANES), 1)
     spare = spare_lanes()
 
@@ -502,15 +526,16 @@
             out[to, :] = out[to, :] + pltpu.roll(v, code & (LANES - 1), 1)
         return carry
 
-    lax.fori_loop(0, 32, place, 0)
+    lax.fori_loop(0, 32, place, 0, unroll=4)
     keep = lane8 < NZ
 
     def unpack(y, carry):
+        first = pl.multiple_of(y * CX * TILE, CX * TILE)
+        for x in range(CX):
+            at = pl.ds(first + x * TILE, TILE)
+            layer[pl.ds(x * TILE, TILE), :] = sum(ref[at, :] for ref in sums)
         for r in range(0, CX, 8):
-            rows = []
-            for k in range(8):
-                at = pl.ds((y * CX + r) * TILE + k, 8, stride=TILE)
-                rows.append(sum(ref[at, :] for ref in sums))
+            rows = [layer[pl.ds(r * TILE + k, 8, stride=TILE), :] for k in range(8)]
             pieces = [pltpu.roll(rows[k], 32 * (k + 1), 1) for k in range(3)]
             ninth = jnp.where(lane8 < 32, pieces[0], jnp.where(lane8 < 64, pieces[1], pieces[2]))
             rows = [jnp.where(keep, v, 0.0) for v in rows[:3]] + rows[3:] + [jnp.where(keep, ninth, 0.0)]
@@ -519,7 +544,7 @@
                     out[c, y, pl.ds(r, 8), :] = rows[3 * i + c]
         return carry
 
-    lax.fori_loop(0, CY, unpack, 0)
+    lax.fori_loop(0, CY, unpack, 0, unroll=4)
 
 
 def scatter(give, vals_a, vals_b, empty):
@@ -530,6 +555,7 @@
         out_shape=[field, field, field] + [table] * COPIES,
         in_specs=[SMEM] + [VMEM] * (2 + COPIES),
         out_specs=[VMEM] * (3 + COPIES),
+        scratch_shapes=[pltpu.VMEM((CX * TILE, LANES), jnp.float32)],
         input_output_aliases={3 + i: 3 + i for i in range(COPIES)},
         compiler_params=pltpu.CompilerParams(vmem_limit_bytes=16 * MIB),
         name="scatter",
@@ -552,7 +578,6 @@
         return carry
 
     lax.fori_loop(0, CY, fill, 0)
-    clear_rims((a3, a2, a1))
     keep = levels()
     inside = inside_grid(*where)
 
@@ -581,6 +606,8 @@
         if n == 0:
             pl.semaphore_wait(barrier, 4)
         copies = send_rims(sides.at[n], inbox.at[n], send.at[n], recv.at[n], *where)
+        if n == 0:
+            clear_rims((a3, a2, a1))
         over_tile(body)
         for copy in copies:
             copy.wait()

time: 81.4 us -> 74.2 us (0.912)
  Pallas kernels: 77.3 us -> 70 us
    pallas_call x1, Pallas kernels: 14.2 us -> 10.7 us  [scatter(): pl.pallas_call(scatter_kernel, out_shape=[field, field, field] + [table]...]
    pallas_call x1, Pallas kernels: 25.8 us -> 23.2 us  [forward(): pl.pallas_call(forward_kernel, out_shape=[wide, wide, wide, table, codes,...]
    pallas_call x1, Pallas kernels: 20.2 us -> 19.1 us  [gather(): pl.pallas_call(gather_kernel, out_shape=[f32(256, LANES), f32(256, LANES)...]
where the time goes in v3:
time: 74.2 us; the launch traced here: 73.9 us
  Pallas kernels  70 us (94%)
  local copies, waits for them, and re-layouts  2.28 us (3%)
  other arithmetic  1.56 us (2%)
    pallas_call x1, Pallas kernels, forward(): pl.pallas_call(forward_kernel, out_shape=[wide, wide, wide, table, codes,...  23.2 us
    pallas_call x1, Pallas kernels, gather(): pl.pallas_call(gather_kernel, out_shape=[f32(256, LANES), f32(256, LANES)...  19.1 us
    pallas_call x1, Pallas kernels, adjoint(): pl.pallas_call(adjoint_kernel, out_shape=f32(3, CX, CY * NZ), in_specs=[V...  17 us
    pallas_call x1, Pallas kernels, scatter(): pl.pallas_call(scatter_kernel, out_shape=[field, field, field] + [table]...  10.7 us
    unnamed x3, local copies, waits for them, and re-layouts  2.28 us

profile of v3, /device:TPU:0, one launch (start us, length us, event | category | flops | bytes accessed | tf_op | source)
XLA Modules:
  0.0 73.9 jit_solution(4744203064856716225)
XLA Ops:
  0.0 0.7 convert_bitcast_fusion
  0.7 0.8 %pad_add_fusion.lists = f32[168,128]{1,0:T(8,128)S(1)} fusion(f32[3,4]{1,0:T(4,128)} %param.6, f32[32,128]{1,0:T(8,128)S(1)} %get-tuple-element.41, f32[96,128]{1,0:T(8,128)} %bitcast.13, f32[32,128]{1,0:T(8,128)S(1)} %get-tuple-element.42), kind=kLoop, calls=%fused_computation | loop fusion | flops 64512 | bytes 167984 | tf_op jit(solution)/shard_map/add | solution.py:655
  1.6 0.0 copy-start
  1.6 1.3 %copy-done = f32[3,32,3072]{2,1,0:T(8,128)S(1)} copy-done((f32[3,32,3072]{2,1,0:T(8,128)S(1)}, f32[3,32,3072]{2,1,0:T(8,128)}, u32[]{:S(2)}) %copy-start) | copy-done | bytes 1179672
  2.8 23.2 %forward.1 = (f32[3,34,48,128]{3,2,1,0:T(8,128)S(1)}, f32[3,34,48,128]{3,2,1,0:T(8,128)S(1)}, f32[3,34,48,128]{3,2,1,0:T(8,128)S(1)}, f32[1024,8,128]{2,1,0:T(8,...) custom-call(f32[3,32,3072]{2,1,0:T(8,128)S(1)} %copy-done, ...), custom_call_target="tpu_custom_call" | custom-call | tf_op jit(solution)/shard_map/forward/pallas_call | solution.py:325
  26.0 19.1 %gather.1 = (f32[256,128]{1,0:T(8,128)S(1)}, f32[256,128]{1,0:T(8,128)S(1)}, f32[8192,128]{1,0:T(8,128)S(1)}, f32[8192,128]{1,0:T(8,128)S(1)}, f32[8192,128]{1,0:T(8,128)S(1)}, /*index=5*/f32[8192,128]{1,0:T(8,128)S(1)}) custom-call(s32[32,128]{1,0:T(8,128)S(1)} %get-tuple-element.27.take, f32[1024,8,128]{2,1,0:T(8,128)S(1)} %get-tuple-element.28.table, ...), custom_call_target="tpu_custom_call" | custom-call | tf_op jit(solution)/shard_map/gather/pallas_call | solution.py:494
  45.1 10.7 %scatter.1 = (f32[3,32,32,128]{3,2,1,0:T(8,128)S(1)}, f32[3,32,32,128]{3,2,1,0:T(8,128)S(1)}, f32[3,32,32,128]{3,2,1,0:T(8,128)S(1)}, f32[8192,128]{1,0:T(8,128)...) custom-call(s32[32,128]{1,0:T(8,128)S(1)} %get-tuple-element.26.give, ...), custom_call_target="tpu_custom_call", output_to_operand_aliasing={{3}: (3, {}), {4}: (4, {}), {5}: (5, {}), {6}: (6, {})} | custom-call | tf_op jit(solution)/shard_map/scatter/pallas_call | solution.py:553
  55.9 17.0 %adjoint.1 = f32[3,32,3072]{2,1,0:T(8,128)S(1)} custom-call(f32[3,34,48,128]{3,2,1,0:T(8,128)S(1)} %get-tuple-element.23.w0, f32[3,34,48,128]{3,2,1,0:T(8,128)S(1)} %get-tuple-element.24.w1, f32[3,34,48,128]{3,2,1,0:T(8,128)S(1)} %get-tuple-element.25.w2, f32[3,32,32,128]{3,2,1,0:T(8,128)S(1)} %get-tuple-element.38.f3, ...), custom_call_target="tpu_custom_call" | custom-call | tf_op jit(solution)/shard_map/adjoint/pallas_call | solution.py:633
  72.9 1.0 %copy.15 = f32[3,32,3072]{2,1,0:T(8,128)} copy(f32[3,32,3072]{2,1,0:T(8,128)S(1)} %adjoint.1) | data formatting | bytes 2359296
Async XLA Ops:
  1.6 1.3 %copy-start = (f32[3,32,3072]{2,1,0:T(8,128)S(1)}, f32[3,32,3072]{2,1,0:T(8,128)}, u32[]{:S(2)}) copy-start(f32[3,32,3072]{2,1,0:T(8,128)} %state.1) | copy-start | bytes 3538948

commit v4 on v3

--- a/solution.py
+++ b/solution.py
@@ -142,11 +142,23 @@
 
 
 def pack_rims(field, sides):
+    keep = levels()
     for s in range(4):
         for c in range(3):
+            v = []
             for y in range(0, CY, 8):
                 ref, at = layer_at(field, s, 0, c, y)
-                sides[s, c, pl.ds(y, 8), :] = ref[at]
+                v.append(ref[at])
+            for k in range(3):
+                sides[s, c, pl.ds(8 * k, 8), :] = jnp.where(keep, v[k], pltpu.roll(v[3], NZ - 32 * k, 1))
+
+
+def rim_rows(inbox, side, c, inside):
+    lane = lax.broadcasted_iota(jnp.int32, (8, LANES), 1)
+    p = [inbox[side, c, pl.ds(8 * k, 8), :] for k in range(3)]
+    q = [pltpu.roll(p[k], 32 * (k + 1), 1) for k in range(3)]
+    p.append(jnp.where(lane < 32, q[0], jnp.where(lane < 64, q[1], q[2])))
+    return [jnp.where((lane < NZ) & inside, v, 0.0) for v in p]
 
 
 def regroup(block, quantity):
@@ -274,16 +286,16 @@
 
     def meet_rims(src, dst, n):
         for s in range(4):
+            factors = []
             for y in range(0, CY, 8):
-                rows = pl.ds(y, 8)
-                speed = sides[n, s, s // 2, rows, :]
-                factor = HALF * (1.0 - speed) if s % 2 else HALF * (1.0 + speed)
-                for c in range(3):
-                    v = jnp.where(inside[s], inbox[n, OPPOSITE[s], c, rows, :], 0.0)
-                    ref, at = layer_at(src, s, 1, c, y)
+                ref, at = layer_at(src, s, 0, s // 2, y)
+                factors.append(HALF * (1.0 - ref[at]) if s % 2 else HALF * (1.0 + ref[at]))
+            for c in range(3):
+                for i, v in enumerate(rim_rows(inbox.at[n], OPPOSITE[s], c, inside[s])):
+                    ref, at = layer_at(src, s, 1, c, 8 * i)
                     ref[at] = v
-                    ref, at = target(dst, s, c, y)
-                    ref[at] = ref[at] + factor * v
+                    ref, at = target(dst, s, c, 8 * i)
+                    ref[at] = ref[at] + factors[i] * v
 
     for n, (src, dst, body) in enumerate(((w0, w1, advance(w0, w1)), (w1, w2, advance(w1, w2)), (w2, None, tables))):
         if n:
@@ -321,7 +333,7 @@
     box = pltpu.VMEM((lax.axis_size("gx"), lax.axis_size("gy"), 2, LANES), jnp.float32)
     wide, table = f32(3, WIDE, ROWS, LANES), f32(CX * CY, TILE, LANES)
     codes = jax.ShapeDtypeStruct((32, LANES), jnp.int32)
-    rim = pltpu.VMEM((STEPS, 4, 3, 32, LANES), jnp.float32)
+    rim = pltpu.VMEM((STEPS, 4, 3, 24, LANES), jnp.float32)
     return pl.pallas_call(
         forward_kernel,
         out_shape=[
@@ -396,7 +408,6 @@
 
     vals_a[...] = jnp.zeros_like(vals_a)
     vals_b[...] = jnp.zeros_like(vals_b)
-    part[...] = jnp.zeros_like(part)
 
     lane8 = lax.broadcasted_iota(jnp.int32, (8, LANES), 1)
     spare = spare_lanes()
@@ -436,7 +447,7 @@
     sums = list_sums(values)
     for i in range(STEPS * BEAMS):
         block = jnp.where(diag, sums[32 * i : 32 * i + 32, :], 0.0)
-        part[pl.ds(i, 1), :] = jnp.sum(block, axis=0, keepdims=True)
+        part[i // BEAMS, pl.ds(i % BEAMS, 1), :] = jnp.sum(block, axis=0, keepdims=True)
     pl.semaphore_wait(barrier, 22)
 
     blank = jnp.zeros((64, LANES), jnp.float32)
@@ -471,7 +482,7 @@
         acc = acc + inbox_b[d]
 
     total = acc * (1.0 / GATES)
-    means = list_sums([jnp.where(diag, total[i : i + 1, :], 0.0) for i in range(STEPS * BEAMS)])
+    means = list_sums([jnp.where(diag, total[i // BEAMS, i % BEAMS : i % BEAMS + 1, :], 0.0) for i in range(STEPS * BEAMS)])
     for n in range(STEPS):
         at = 32 * BEAMS * n
         mean = jnp.zeros((32, LANES), jnp.float32)
@@ -490,7 +501,7 @@
 
 def gather(take, table, third, slots, seen_obs):
     rows = pltpu.VMEM((256, LANES), jnp.float32)
-    block = pltpu.VMEM((16, LANES), jnp.float32)
+    block = pltpu.VMEM((STEPS, BEAMS, LANES), jnp.float32)
     return pl.pallas_call(
         gather_kernel,
         out_shape=[f32(256, LANES), f32(256, LANES)] + [f32(CX * CY * TILE, LANES)] * COPIES,
@@ -498,7 +509,7 @@
         out_specs=[VMEM] * (2 + COPIES),
         scratch_shapes=[
             rows, rows, pltpu.VMEM((STEPS, 32, LANES), jnp.float32), block, block,
-            pltpu.VMEM((7, 16, LANES), jnp.float32), pltpu.VMEM((15, 16, LANES), jnp.float32),
+            pltpu.VMEM((7, STEPS, BEAMS, LANES), jnp.float32), pltpu.VMEM((15, STEPS, BEAMS, LANES), jnp.float32),
             pltpu.SemaphoreType.DMA((7,)), pltpu.SemaphoreType.DMA((7,)),
             pltpu.SemaphoreType.DMA((15,)), pltpu.SemaphoreType.DMA((15,)),
         ],
@@ -583,13 +594,14 @@
 
     def meet_rims(src, dst, n):
         for s in range(4):
+            factors = []
             for y in range(0, CY, 8):
                 ref, at = layer_at(src, s, 1, s // 2, y)
-                factor = HALF * (1.0 + ref[at]) if s % 2 else HALF * (1.0 - ref[at])
-                for c in range(3):
-                    v = jnp.where(inside[s], inbox[n, OPPOSITE[s], c, pl.ds(y, 8), :], 0.0)
-                    ref, at = layer_at(dst, s, 0, c, y)
-                    ref[at] = ref[at] + factor * v
+                factors.append(HALF * (1.0 + ref[at]) if s % 2 else HALF * (1.0 - ref[at]))
+            for c in range(3):
+                for i, v in enumerate(rim_rows(inbox.at[n], OPPOSITE[s], c, inside[s])):
+                    ref, at = layer_at(dst, s, 0, c, 8 * i)
+                    ref[at] = ref[at] + factors[i] * v
 
     def pull(src, adj, dst, force):
         def body(y, r):
@@ -629,7 +641,7 @@
 
 def adjoint(wides, fields):
     wide = pltpu.VMEM((3, WIDE, ROWS, LANES), jnp.float32)
-    rim = pltpu.VMEM((STEPS, 4, 3, 32, LANES), jnp.float32)
+    rim = pltpu.VMEM((STEPS, 4, 3, 24, LANES), jnp.float32)
     return pl.pallas_call(
         adjoint_kernel,
         out_shape=f32(3, CX, CY * NZ),
@@ -652,9 +664,8 @@
         return jnp.pad(block, ((first, rows - first - block.shape[0]), (0, count - block.shape[1])))
 
     lists = (
-        at_row(slot_cell[0].T.astype(jnp.float32), 0)
+        (at_row(slot_cell[0].T, 0) + at_row(slot_beam[0].T, 4 * capacity)).astype(jnp.float32)
         + at_row(jnp.transpose(gate_obs[:, 0], (0, 2, 1)).reshape(-1, count), capacity)
-        + at_row(slot_beam[0].T.astype(jnp.float32), 4 * capacity)
         + at_row(beam_dir, 5 * capacity)
     )
     w0, w1, w2, table, take, give, third, slots, seen_obs = forward(initial_state, lists)

time: 74.2 us -> 71.6 us (0.965)
  Pallas kernels: 70 us -> 68.3 us
    pallas_call x1, Pallas kernels: 19.1 us -> 17.8 us  [gather(): pl.pallas_call(gather_kernel, out_shape=[f32(256, LANES), f32(256, LANES)...]
where the time goes in v4:
time: 71.6 us; the launch traced here: 71.4 us
  Pallas kernels  68.3 us (95%)
  local copies, waits for them, and re-layouts  2.28 us (3%)
  other arithmetic  0.82 us (1%)
    pallas_call x1, Pallas kernels, forward(): pl.pallas_call(forward_kernel, out_shape=[wide, wide, wide, table, codes,...  22.5 us
    pallas_call x1, Pallas kernels, gather(): pl.pallas_call(gather_kernel, out_shape=[f32(256, LANES), f32(256, LANES)...  17.8 us
    pallas_call x1, Pallas kernels, adjoint(): pl.pallas_call(adjoint_kernel, out_shape=f32(3, CX, CY * NZ), in_specs=[V...  17.3 us
    pallas_call x1, Pallas kernels, scatter(): pl.pallas_call(scatter_kernel, out_shape=[field, field, field] + [table]...  10.7 us
    unnamed x3, local copies, waits for them, and re-layouts  2.28 us

profile of v4, /device:TPU:0, one launch (start us, length us, event | category | flops | bytes accessed | tf_op | source)
XLA Modules:
  0.0 71.4 jit_solution(11598563481115198924)
XLA Ops:
  0.0 0.8 %pad_add_fusion.lists = f32[168,128]{1,0:T(8,128)S(1)} fusion(f32[3,4]{1,0:T(4,128)} %param.6, f32[96,128]{1,0:T(8,128)} %bitcast.11, s32[32,128]{1,0:T(8,128)} %bitcast.12, s32[32,128]{1,0:T(8,128)} %bitcast.13), kind=kLoop, calls=%fused_computation | loop fusion | flops 86016 | bytes 167984 | tf_op jit(solution)/shard_map/add | solution.py:667
  0.8 0.0 copy-start
  0.8 1.3 %copy-done = f32[3,32,3072]{2,1,0:T(8,128)S(1)} copy-done((f32[3,32,3072]{2,1,0:T(8,128)S(1)}, f32[3,32,3072]{2,1,0:T(8,128)}, u32[]{:S(2)}) %copy-start) | copy-done | bytes 1179672
  2.1 22.5 %forward.1 = (f32[3,34,48,128]{3,2,1,0:T(8,128)S(1)}, f32[3,34,48,128]{3,2,1,0:T(8,128)S(1)}, f32[3,34,48,128]{3,2,1,0:T(8,128)S(1)}, f32[1024,8,128]{2,1,0:T(8,...) custom-call(f32[3,32,3072]{2,1,0:T(8,128)S(1)} %copy-done, ...), custom_call_target="tpu_custom_call" | custom-call | tf_op jit(solution)/shard_map/forward/pallas_call | solution.py:337
  24.6 17.8 %gather.1 = (f32[256,128]{1,0:T(8,128)S(1)}, f32[256,128]{1,0:T(8,128)S(1)}, f32[8192,128]{1,0:T(8,128)S(1)}, f32[8192,128]{1,0:T(8,128)S(1)}, f32[8192,128]{1,0:T(8,128)S(1)}, /*index=5*/f32[8192,128]{1,0:T(8,128)S(1)}) custom-call(s32[32,128]{1,0:T(8,128)S(1)} %get-tuple-element.27.take, f32[1024,8,128]{2,1,0:T(8,128)S(1)} %get-tuple-element.28.table, ...), custom_call_target="tpu_custom_call" | custom-call | tf_op jit(solution)/shard_map/gather/pallas_call | solution.py:505
  42.4 10.7 %scatter.1 = (f32[3,32,32,128]{3,2,1,0:T(8,128)S(1)}, f32[3,32,32,128]{3,2,1,0:T(8,128)S(1)}, f32[3,32,32,128]{3,2,1,0:T(8,128)S(1)}, f32[8192,128]{1,0:T(8,128)...) custom-call(s32[32,128]{1,0:T(8,128)S(1)} %get-tuple-element.26.give, ...), custom_call_target="tpu_custom_call", output_to_operand_aliasing={{3}: (3, {}), {4}: (4, {}), {5}: (5, {}), {6}: (6, {})} | custom-call | tf_op jit(solution)/shard_map/scatter/pallas_call | solution.py:564
  53.1 17.3 %adjoint.1 = f32[3,32,3072]{2,1,0:T(8,128)S(1)} custom-call(f32[3,34,48,128]{3,2,1,0:T(8,128)S(1)} %get-tuple-element.23.w0, f32[3,34,48,128]{3,2,1,0:T(8,128)S(1)} %get-tuple-element.24.w1, f32[3,34,48,128]{3,2,1,0:T(8,128)S(1)} %get-tuple-element.25.w2, f32[3,32,32,128]{3,2,1,0:T(8,128)S(1)} %get-tuple-element.38.f3, ...), custom_call_target="tpu_custom_call" | custom-call | tf_op jit(solution)/shard_map/adjoint/pallas_call | solution.py:645
  70.4 1.0 %copy.15 = f32[3,32,3072]{2,1,0:T(8,128)} copy(f32[3,32,3072]{2,1,0:T(8,128)S(1)} %adjoint.1) | data formatting | bytes 2359296
Async XLA Ops:
  0.8 1.3 %copy-start = (f32[3,32,3072]{2,1,0:T(8,128)S(1)}, f32[3,32,3072]{2,1,0:T(8,128)}, u32[]{:S(2)}) copy-start(f32[3,32,3072]{2,1,0:T(8,128)} %state.1) | copy-start | bytes 3538948

commit v5 on v4

--- a/solution.py
+++ b/solution.py
@@ -174,12 +174,17 @@
 
 
 def forward_kernel(
-    state, lists,
+    state_in, cell_in, obs_in, beam_in, dir_in,
     w0, w1, w2, table, take, give, third, slots, seen_obs,
-    got, mid, msg, sides, inbox, send, recv, list_send, list_recv, own,
+    state, cell, obs, beam, beam_dir, load, got, mid, msg, sides, inbox, send, recv, list_send, list_recv, own,
 ):
     n_gx, n_gy, gx, gy = sizes()
     barrier = pltpu.get_barrier_semaphore()
+    loads = []
+    pairs = ((state_in, state), (cell_in, cell), (obs_in, obs), (beam_in, beam), (dir_in, beam_dir))
+    for i, (src, dst) in enumerate(pairs):
+        loads.append(pltpu.make_async_copy(src, dst, load.at[i]))
+        loads[-1].start()
 
     def along_x(i):
         to = lax.rem(gx + i, n_gx)
@@ -197,6 +202,8 @@
 
     lax.fori_loop(1, n_gx, hail(along_x), 0)
     lax.fori_loop(1, n_gy, hail(along_y), 0)
+    for copy in loads:
+        copy.wait()
     lane = lax.broadcasted_iota(jnp.int32, (CX, LANES), 1)
     for c in range(3):
         for y in range(0, CY, 4):
@@ -214,15 +221,15 @@
 
     where = (n_gx, n_gy, gx, gy)
     copies = send_rims(sides.at[0], inbox.at[0], send.at[0], recv.at[0], *where)
-    kind = lists[pl.ds(LANES, 32), :]
-    tails = [kind]
-    beam_dir = lists[pl.ds(LANES + 32, 8), :]
+    kind = beam[...]
+    heads = [cell[...].astype(jnp.float32), obs[0], obs[1], obs[2]]
+    tails = [kind.astype(jnp.float32)]
     for c in range(3):
         weight = jnp.zeros(kind.shape, jnp.float32)
         for b in range(BEAMS):
-            weight = jnp.where(kind == float(b), beam_dir[c : c + 1, b : b + 1], weight)
+            weight = jnp.where(kind == b, beam_dir[c, b], weight)
         tails.append(weight)
-    msg[:, :, 0, :] = lists[pl.ds(0, LANES), :].T.reshape(n_gx, n_gy, LANES)
+    msg[:, :, 0, :] = jnp.concatenate(heads, axis=0).T.reshape(n_gx, n_gy, LANES)
     msg[:, :, 1, :] = jnp.concatenate(tails, axis=0).T.reshape(n_gx, n_gy, LANES)
 
 
@@ -329,7 +336,7 @@
         seen_obs[n] = regroup(g0, 1 + n)
 
 
-def forward(state, lists):
+def forward(*inputs):
     box = pltpu.VMEM((lax.axis_size("gx"), lax.axis_size("gy"), 2, LANES), jnp.float32)
     wide, table = f32(3, WIDE, ROWS, LANES), f32(CX * CY, TILE, LANES)
     codes = jax.ShapeDtypeStruct((32, LANES), jnp.int32)
@@ -339,16 +346,18 @@
         out_shape=[
             wide, wide, wide, table, codes, codes, f32(32, LANES), f32(4, 32, LANES), f32(STEPS, 32, LANES),
         ],
-        in_specs=[VMEM] * 2,
+        in_specs=[pl.BlockSpec(memory_space=pltpu.HBM)] * 5,
         out_specs=[VMEM] * 9,
         scratch_shapes=[
+            *[pltpu.VMEM(v.shape, v.dtype) for v in inputs[:4]], pltpu.SMEM(inputs[4].shape, jnp.float32),
+            pltpu.SemaphoreType.DMA((5,)),
             box, box, box, rim, rim,
             pltpu.SemaphoreType.DMA((STEPS, 4)), pltpu.SemaphoreType.DMA((STEPS, 4)),
             pltpu.SemaphoreType.DMA((2,)), pltpu.SemaphoreType.DMA((2,)), pltpu.SemaphoreType.DMA((2,)),
         ],
         compiler_params=pltpu.CompilerParams(collective_id=0, has_side_effects=True, vmem_limit_bytes=24 * MIB),
         name="forward",
-    )(state, lists)
+    )(*[pltpu.with_memory_space_constraint(v, pltpu.HBM) for v in inputs])
 
 
 def spare_lanes():
@@ -656,19 +665,9 @@
 
 
 def local(initial_state, beam_dir, gate_obs, slot_beam, slot_cell):
-    count = slot_cell.shape[1]
-    capacity = slot_cell.shape[2]
-    rows = 5 * capacity + 8
-
-    def at_row(block, first):
-        return jnp.pad(block, ((first, rows - first - block.shape[0]), (0, count - block.shape[1])))
-
-    lists = (
-        (at_row(slot_cell[0].T, 0) + at_row(slot_beam[0].T, 4 * capacity)).astype(jnp.float32)
-        + at_row(jnp.transpose(gate_obs[:, 0], (0, 2, 1)).reshape(-1, count), capacity)
-        + at_row(beam_dir, 5 * capacity)
+    w0, w1, w2, table, take, give, third, slots, seen_obs = forward(
+        initial_state, slot_cell[0].T, jnp.transpose(gate_obs[:, 0], (0, 2, 1)), slot_beam[0].T, beam_dir
     )
-    w0, w1, w2, table, take, give, third, slots, seen_obs = forward(initial_state, lists)
     vals_a, vals_b, *empty = gather(take, table, third, slots, seen_obs)
     fields = scatter(give, vals_a, vals_b, empty)
     return adjoint((w0, w1, w2), fields)

time: 71.6 us -> 69.6 us (0.972)
  local copies, waits for them, and re-layouts: 2.28 us -> 1.02 us
  other arithmetic: 0.82 us -> 0 us
    unnamed x3 -> x1, local copies, waits for them, and re-layouts: 2.28 us -> 1.02 us
    add x1 -> x0, other arithmetic: 0.82 us -> none  [local(): (at_row(slot_cell[0].T, 0) + at_row(slot_beam[0].T, 4 * capacity)).astype...]
where the time goes in v5:
time: 69.6 us; the launch traced here: 69.3 us
  Pallas kernels  68.3 us (98%)
  local copies, waits for them, and re-layouts  1.02 us (1%)
    pallas_call x1, Pallas kernels, forward(): pl.pallas_call(forward_kernel, out_shape=[wide, wide, wide, table, codes,...  22.7 us
    pallas_call x1, Pallas kernels, gather(): pl.pallas_call(gather_kernel, out_shape=[f32(256, LANES), f32(256, LANES)...  17.8 us
    pallas_call x1, Pallas kernels, adjoint(): pl.pallas_call(adjoint_kernel, out_shape=f32(3, CX, CY * NZ), in_specs=[V...  17.1 us
    pallas_call x1, Pallas kernels, scatter(): pl.pallas_call(scatter_kernel, out_shape=[field, field, field] + [table]...  10.7 us

profile of v5, /device:TPU:0, one launch (start us, length us, event | category | flops | bytes accessed | tf_op | source)
XLA Modules:
  0.0 69.3 jit_solution(17159618175771819326)
XLA Ops:
  0.0 22.7 %forward.1 = (f32[3,34,48,128]{3,2,1,0:T(8,128)S(1)}, f32[3,34,48,128]{3,2,1,0:T(8,128)S(1)}, f32[3,34,48,128]{3,2,1,0:T(8,128)S(1)}, f32[1024,8,128]{2,1,0:T(8,...) custom-call(f32[3,32,3072]{2,1,0:T(8,128)} %state_in.1, ...), custom_call_target="tpu_custom_call" | custom-call | tf_op jit(solution)/shard_map/forward/pallas_call | solution.py:344
  22.7 17.8 %gather.1 = (f32[256,128]{1,0:T(8,128)S(1)}, f32[256,128]{1,0:T(8,128)S(1)}, f32[8192,128]{1,0:T(8,128)S(1)}, f32[8192,128]{1,0:T(8,128)S(1)}, f32[8192,128]{1,0:T(8,128)S(1)}, /*index=5*/f32[8192,128]{1,0:T(8,128)S(1)}) custom-call(s32[32,128]{1,0:T(8,128)S(1)} %get-tuple-element.27.take, f32[1024,8,128]{2,1,0:T(8,128)S(1)} %get-tuple-element.28.table, ...), custom_call_target="tpu_custom_call" | custom-call | tf_op jit(solution)/shard_map/gather/pallas_call | solution.py:514
  40.5 10.7 %scatter.1 = (f32[3,32,32,128]{3,2,1,0:T(8,128)S(1)}, f32[3,32,32,128]{3,2,1,0:T(8,128)S(1)}, f32[3,32,32,128]{3,2,1,0:T(8,128)S(1)}, f32[8192,128]{1,0:T(8,128)...) custom-call(s32[32,128]{1,0:T(8,128)S(1)} %get-tuple-element.26.give, ...), custom_call_target="tpu_custom_call", output_to_operand_aliasing={{3}: (3, {}), {4}: (4, {}), {5}: (5, {}), {6}: (6, {})} | custom-call | tf_op jit(solution)/shard_map/scatter/pallas_call | solution.py:573
  51.2 17.1 %adjoint.1 = f32[3,32,3072]{2,1,0:T(8,128)S(1)} custom-call(f32[3,34,48,128]{3,2,1,0:T(8,128)S(1)} %get-tuple-element.23.w0, f32[3,34,48,128]{3,2,1,0:T(8,128)S(1)} %get-tuple-element.24.w1, f32[3,34,48,128]{3,2,1,0:T(8,128)S(1)} %get-tuple-element.25.w2, f32[3,32,32,128]{3,2,1,0:T(8,128)S(1)} %get-tuple-element.38.f3, ...), custom_call_target="tpu_custom_call" | custom-call | tf_op jit(solution)/shard_map/adjoint/pallas_call | solution.py:654
  68.3 1.0 %copy.15 = f32[3,32,3072]{2,1,0:T(8,128)} copy(f32[3,32,3072]{2,1,0:T(8,128)S(1)} %adjoint.1) | data formatting | bytes 2359296
